TPU v7x, 512 devices: a whole 4x8x8 slice. The times are simulated.
512 devices in a mesh: dp: 8 (over y), seq: 64 (over z, x, core).
Axes of the slice: x: 4, y: 8, z: 8, core: 2. Of those that a mesh axis runs over, the one named last changes fastest.
Arguments:
- queries: bfloat16 [8, 8192, 1536], P('dp', 'seq'), may hold values from -6 to 6
- keys: bfloat16 [8, 8192, 1536], P('dp', 'seq'), may hold values from -6 to 6
- values: bfloat16 [8, 8192, 1536], P('dp', 'seq'), may hold values from -6 to 6
- segment_ids: int32 [8, 8192], P('dp'), may hold values from 0 to 127, never falling along the last dimension, each value on 1 to 128 neighbouring positions
- norm_gain: float32 [1536], replicated, may hold values from 0.25 to 1.75
- conv_kernel: float32 [31, 1536], replicated, may hold values from -1 to 1
- conv_bias: float32 [1536], replicated, may hold values from -3 to 3
- cotangent: bfloat16 [8, 8192, 1536], P('dp', 'seq'), may hold values from -6 to 6
Outputs:
- conv_out: bfloat16 [8, 8192, 1536], P('dp', 'seq')
- query_grad: bfloat16 [8, 8192, 1536], P('dp', 'seq')
- key_grad: bfloat16 [8, 8192, 1536], P('dp', 'seq')
- value_grad: bfloat16 [8, 8192, 1536], P('dp', 'seq')
- gain_grad: float32 [1536], replicated
- kernel_grad: float32 [31, 1536], replicated
- bias_grad: float32 [1536], replicated
Inputs may be any that keep to these rules, and one draw needn't show every extreme that they name: `segment_ids`: within each row, utterance numbers never fall; each utterance holds 1 to 128 frames, and some utterance exactly 128.
All inputs are finite; a program needn't handle non-finite values.
Results may differ from a plain program's by a relative error of at most 0.023.
Values may be sent and summed in bfloat16 or wider, within the bound.
A program may use at most 64 MiB of HBM per device.

v0:
```python
import jax
import jax.numpy as jnp
from jax import lax
from jax.sharding import PartitionSpec as P

HEADS = 24
HEAD_DIM = 64
HEAD_BLOCK = 4
REACH = 1


EPS = 1e-05
NEG = -1e30


def shifted(block, axis, distance):
    devices = range(lax.axis_size(axis))
    route = [(i - distance, i) for i in devices if i - distance in devices]
    return lax.ppermute(block, axis, route)


def with_halo(cells, sides, width):
    for axis, dim in sides:
        count = lax.axis_size(axis)
        ends = count - 1
        head = lax.slice_in_dim(cells, 0, width, axis=dim)
        tail = lax.slice_in_dim(cells, cells.shape[dim] - width, cells.shape[dim], axis=dim)
        cells = jnp.concatenate(
            [
                lax.ppermute(tail, axis, [(i, (i + 1) % count) for i in range(ends)]),
                cells,
                lax.ppermute(head, axis, [((i + 1) % count, i) for i in range(ends)]),
            ],
            axis=dim,
        )
    return cells


def to_groups(tensor, block):
    rows_in, heads_in, dim_in = tensor.shape
    return tensor.reshape(rows_in, heads_in // block, block, dim_in).transpose(1, 0, 2, 3)


def from_groups(tensor):
    groups_in, rows_in, block, dim_in = tensor.shape
    return tensor.transpose(1, 0, 2, 3).reshape(rows_in, groups_in * block * dim_in)


def masked_logits(query_rows, key_rows, same_seg):
    factor = query_rows.shape[-1] ** (-0.5)
    logits = (
        jnp.einsum("qhe,khe->hqk", query_rows, key_rows, preferred_element_type=jnp.float32)
        * factor
    )
    return jnp.where(same_seg[None], logits, NEG)


def forward_block(query_rows, key_rows, value_rows, same_seg):
    logits = masked_logits(query_rows, key_rows, same_seg)
    row_top = jnp.max(logits, -1, keepdims=True)
    exponent = jnp.exp(logits - row_top)
    row_total = jnp.sum(exponent, -1, keepdims=True)
    attn_weights = (exponent / row_total).astype(jnp.bfloat16)
    context = jnp.einsum(
        "hqk,khe->qhe", attn_weights, value_rows, preferred_element_type=jnp.float32
    )
    return (context, (row_top + jnp.log(row_total))[..., 0])


def back_terms(query_rows, key_rows, value_rows, grad_rows, log_total, row_delta, same_seg):
    factor = query_rows.shape[-1] ** (-0.5)
    logits = masked_logits(query_rows, key_rows, same_seg)
    prob_back = jnp.exp(logits - log_total[:, :, None])
    grad_prob = jnp.einsum(
        "qhe,khe->hqk", grad_rows, value_rows, preferred_element_type=jnp.float32
    )
    grad_logit = (prob_back * (grad_prob - row_delta[:, :, None]) * factor).astype(jnp.bfloat16)
    return (prob_back.astype(jnp.bfloat16), grad_logit)


def per_device(queries, keys, values, segment_ids, norm_gain, conv_kernel, conv_bias, cotangent):
    frame_count = queries.shape[1]
    width = queries.shape[2]
    reach_rows = REACH * frame_count
    tap_count = conv_kernel.shape[0]
    half_taps = tap_count // 2
    block = HEAD_BLOCK
    group_count = HEADS // block
    start_row = lax.axis_index("seq") * frame_count
    seg_row = segment_ids[0]
    seg_padded = jnp.pad(seg_row, (reach_rows, reach_rows), constant_values=-1)
    own_seg = lax.dynamic_slice_in_dim(seg_row, start_row, frame_count)
    window_seg = lax.dynamic_slice_in_dim(seg_padded, start_row, frame_count + 2 * reach_rows)
    conv_seg = lax.dynamic_slice_in_dim(
        seg_padded, start_row + reach_rows - half_taps, frame_count + 2 * half_taps
    )
    same_fwd = own_seg[:, None] == window_seg[None, :]
    query_heads = queries[0].reshape(frame_count, HEADS, HEAD_DIM)
    key_value = jnp.stack((keys[0], values[0]), 1)
    lower_parts = []
    upper_parts = []
    hop = 1
    for offset_by in (hop, -hop):
        arrived = shifted(key_value, "seq", offset_by)
        if offset_by > 0:
            lower_parts.insert(0, arrived)
        else:
            upper_parts.append(arrived)
    key_value_wide = jnp.concatenate(lower_parts + [key_value] + upper_parts, 0)
    query_groups = to_groups(query_heads, block)
    key_groups = to_groups(key_value_wide[:, 0].reshape(-1, HEADS, HEAD_DIM), block)
    value_groups = to_groups(key_value_wide[:, 1].reshape(-1, HEADS, HEAD_DIM), block)

    def forward_group(operands):
        return forward_block(operands[0], operands[1], operands[2], same_fwd)

    context_groups, total_groups = lax.map(forward_group, (query_groups, key_groups, value_groups))
    context = from_groups(context_groups).astype(jnp.bfloat16)
    context_f = context.astype(jnp.float32)
    row_mean = jnp.mean(context_f, -1, keepdims=True)
    centred = context_f - row_mean
    inv_std = lax.rsqrt(jnp.mean(centred * centred, -1, keepdims=True) + EPS)
    normed = centred * inv_std
    conv_in = (normed * norm_gain).astype(jnp.bfloat16)
    conv_wide = with_halo(conv_in, (("seq", 0),), half_taps).astype(jnp.float32)
    same_taps = [
        (conv_seg[tap_index : tap_index + frame_count] == own_seg)[:, None]
        for tap_index in range(tap_count)
    ]
    pre_act = jnp.broadcast_to(conv_bias, (frame_count, width))
    for tap_index in range(tap_count):
        pre_act = pre_act + conv_kernel[tap_index] * jnp.where(
            same_taps[tap_index], conv_wide[tap_index : tap_index + frame_count], 0.0
        )
    gate_sig = jax.nn.sigmoid(pre_act)
    conv_out = (pre_act * gate_sig).astype(jnp.bfloat16)
    grad_pre = (
        cotangent[0].astype(jnp.float32) * gate_sig * (1.0 + pre_act * (1.0 - gate_sig))
    ).astype(jnp.bfloat16)
    grad_pre_f = grad_pre.astype(jnp.float32)
    bias_part = jnp.sum(grad_pre_f, 0)
    kernel_rows = []
    for tap_index in range(tap_count):
        kernel_rows.append(
            jnp.sum(
                jnp.where(
                    same_taps[tap_index],
                    conv_wide[tap_index : tap_index + frame_count] * grad_pre_f,
                    0.0,
                ),
                0,
            )
        )
    kernel_part = jnp.stack(kernel_rows, 0)
    grad_wide = with_halo(grad_pre, (("seq", 0),), half_taps).astype(jnp.float32)
    grad_in = jnp.zeros((frame_count, width), jnp.float32)
    for tap_index in range(tap_count):
        mirror = 2 * half_taps - tap_index
        grad_in = grad_in + conv_kernel[tap_index] * jnp.where(
            same_taps[mirror], grad_wide[mirror : mirror + frame_count], 0.0
        )
    gain_part = jnp.sum(grad_in * normed, 0)
    grad_norm = grad_in * norm_gain
    grad_context = (
        (
            grad_norm
            - jnp.mean(grad_norm, -1, keepdims=True)
            - normed * jnp.mean(grad_norm * normed, -1, keepdims=True)
        )
        * inv_std
    ).astype(jnp.bfloat16)
    row_delta = jnp.sum(
        (grad_context.astype(jnp.float32) * context_f).reshape(frame_count, HEADS, HEAD_DIM), -1
    )
    delta_groups = row_delta.T.reshape(group_count, block, frame_count)
    grad_groups = to_groups(grad_context.reshape(frame_count, HEADS, HEAD_DIM), block)

    def backward_group(operands):
        query_rows, key_rows, value_rows, grad_rows, log_total, delta_rows = operands
        prob_low, grad_logit = back_terms(
            query_rows, key_rows, value_rows, grad_rows, log_total, delta_rows, same_fwd
        )
        query_part = jnp.einsum(
            "hqk,khe->qhe", grad_logit, key_rows, preferred_element_type=jnp.float32
        )
        key_part = jnp.einsum(
            "hqk,qhe->khe", grad_logit, query_rows, preferred_element_type=jnp.float32
        )
        value_part = jnp.einsum(
            "hqk,qhe->khe", prob_low, grad_rows, preferred_element_type=jnp.float32
        )
        return (query_part, key_part, value_part)

    query_blocks, key_blocks, value_blocks = lax.map(
        backward_group,
        (query_groups, key_groups, value_groups, grad_groups, total_groups, delta_groups),
    )
    key_value_grad = jnp.stack((from_groups(key_blocks), from_groups(value_blocks)), 1)
    own_grad = key_value_grad[reach_rows : reach_rows + frame_count]
    hop = 1
    for offset_by in (hop, -hop):
        if offset_by > 0:
            moved_piece = key_value_grad[
                (REACH + hop) * frame_count : (REACH + hop + 1) * frame_count
            ]
        else:
            moved_piece = key_value_grad[
                (REACH - hop) * frame_count : (REACH - hop + 1) * frame_count
            ]
        own_grad = own_grad + shifted(moved_piece.astype(jnp.bfloat16), "seq", offset_by).astype(
            moved_piece.dtype
        )
    key_grad = own_grad[:, 0]
    value_grad = own_grad[:, 1]
    query_grad = from_groups(query_blocks)
    gain_sum, kernel_sum, bias_sum = lax.psum((gain_part, kernel_part, bias_part), ("dp", "seq"))
    norm_factor = (lax.axis_size("dp") * lax.axis_size("seq") * frame_count) ** (-0.5)
    return (
        conv_out[None],
        query_grad.astype(jnp.bfloat16)[None],
        key_grad.astype(jnp.bfloat16)[None],
        value_grad.astype(jnp.bfloat16)[None],
        gain_sum * norm_factor,
        kernel_sum * norm_factor,
        bias_sum * norm_factor,
    )


def solution(mesh):
    placed = (
        P("dp", "seq", None),
        P("dp", "seq", None),
        P("dp", "seq", None),
        P("dp", None),
        P(),
        P(),
        P(),
        P("dp", "seq", None),
    )
    return jax.shard_map(
        per_device,
        mesh=mesh,
        in_specs=placed,
        out_specs=(
            P("dp", "seq", None),
            P("dp", "seq", None),
            P("dp", "seq", None),
            P("dp", "seq", None),
            P(),
            P(),
            P(),
        ),
        check_vma=False,
    )
```

profile of v0, /device:TPU:1, one launch (start us, length us, event | category | flops | bytes accessed | tf_op | source)
XLA Modules:
  0.0 418.6 jit_solution(15522786637393165617)
XLA Ops:
  7.2 1.3 pad_maximum_fusion.2
  8.5 8.7 %collective-permute-start.1 = (bf16[128,2,1536]{2,0,1:T(8,128)(2,1)S(1)}, bf16[128,2,1536]{2,0,1:T(8,128)(2,1)S(1)}, u32[]{:S(2)}, u32[]{:S(2)}) collective-permute-start(bf16[128,2,1536]{2,0,1:T(8,128)(2,1)S(1)} %pad_maximum_fusion.2), channel_id=1, source_target_pairs={{1,0},{2,1},{3,2},{4,3},{5,4},{6,5},{7,6},{8,7},{9,8},{10,9},{11,1... | collective-permute-start | bytes 2359304 | tf_op jit(solution)/shard_map/ppermute | solution.py:19
  17.3 1.9 collective-permute-start
  19.2 2.5 slice_reduce_fusion.30
  26.3 1.8 collective-permute-done
  29.2 1.4 copy.23
  30.7 21.4 %while.28 = (s32[]{:T(128)}, bf16[6,128,4,64]{1,3,2,0:T(8,128)(2,1)S(1)}, f32[6,4,128]{2,1,0:T(4,128)}, bf16[6,384,4,64]{1,3,2,0:T(8,128)(2,1)}, bf16[6,128,4,64...) while((s32[]{:T(128)}, ...), condition=%wide.region_3.4_spmd.clone, body=%wide.region_0.3_spmd.clone.sunk | while | flops 51953152 | bytes 3068009 | solution.py:117
  30.8 1.2 fusion.223
  32.4 1.3 fusion.225
  34.4 1.2 fusion.223
  35.9 1.3 fusion.225
  37.9 1.2 fusion.223
  39.5 1.3 fusion.225
  41.5 1.2 fusion.223
  43.0 1.3 fusion.225
  45.1 1.2 fusion.223
  46.6 1.3 fusion.225
  48.6 1.2 fusion.223
  50.2 1.3 fusion.225
  53.9 4.4 %collective-permute-start.2 = (bf16[15,1536]{0,1:T(8,128)(2,1)}, bf16[15,1536]{0,1:T(8,128)(2,1)}, u32[]{:S(2)}, u32[]{:S(2)}) collective-permute-start(bf16[15,1536]{0,1:T(8,128)(2,1)} %get-tuple-element.291), channel_id=1, source_target_pairs={{0,1},{1,2},{2,3},{3,4},{4,5},{5,6},{6,7},{7,8},{8,9},{9,10},{10,1... | collective-permute-start | bytes 138248 | tf_op jit(solution)/shard_map/ppermute | solution.py:30
  58.3 2.1 collective-permute-start.3
  60.4 2.1 slice_reduce_fusion.29
  64.1 3.6 collective-permute-done.3
  67.7 1.6 maximum_convert_fusion
  69.6 18.6 %fusion.110 = (f32[1536]{0:T(1024)S(1)}, f32[1536]{0:T(1024)S(1)}, f32[1536]{0:T(1024)S(1)}, f32[1536]{0:T(1024)S(1)}, f32[1536]{0:T(1024)S(1)}, /*index=5*/f32[...) fusion(f32[158,1536]{0,1:T(8,128)S(1)} %maximum_convert_fusion,, ...), kind=kLoop, calls=%fused_computation.158 | loop fusion | flops 25741824 | bytes 26208128 | tf_op jit(solution)/shard_map/reduce_sum | solution.py:145
  88.3 4.4 %fusion.112 = (f32[1536]{0:T(1024)S(1)}, f32[1536]{0:T(1024)S(1)}, f32[1536]{0:T(1024)S(1)}, f32[1536]{0:T(1024)S(1)}, f32[1536]{0:T(1024)S(1)}, /*index=5*/f32[...) fusion(bf16[128,1536]{0,1:T(8,128)(2,1)S(1)} %get-tuple-element.272, ...), kind=kLoop, calls=%fused_computation.160 | loop fusion | flops 5491200 | bytes 7527552 | tf_op jit(solution)/shard_map/reduce_sum | solution.py:145
  92.8 3.7 fusion.114
  97.5 1.9 collective-permute-start.4
  99.4 3.4 collective-permute-start.5
  102.8 2.2 fusion.108
  123.5 6.0 %stack.135 = f32[31,1536]{1,0:T(8,128)} concatenate(f32[1,1536]{1,0:T(1,128)} %stack.104, f32[1,1536]{1,0:T(1,128)} %stack.105, f32[1,1536]{1,0:T(1,128)} %stack.106, f32[1,1536]{1,0:T(1,128)} %stack.107, f32[1,1536]{1,0:T(1,128)} %stack.108, f32[1,1536]{1,0:T(1,128)} %stack.109, f32[1,1536]{1,0:T(1,128)} %stack.110, f32[1,1536]{1,0:T(1,128)} %stack.111, f32[1,1536]{1,0:T(1,128)} %stack.112, ...), dimensions={0} | concatenate | bytes 380928 | tf_op jit(solution)/shard_map/stack | solution.py:154
  129.5 1.6 maximum_convert_fusion.1
  131.1 19.2 %fusion.190 = (f32[1536]{0:T(1024)}, f32[128]{0:T(128)S(1)}, f32[128]{0:T(128)S(1)}, f32[128,1536]{0,1:T(8,128)S(1)}) fusion(bf16[6,128,4,64]{1,3,2,0:T(8,128)(2,1)S(1)} %get-tuple-element.104, f32[128]{0:T(128)} %copy-done.59, f32[128]{0:T(128)} %copy-done.57, f32[1536]{0:T(1024)} %param.16, f32[158,1536]{0,1:T(8,128)S(1)} %maximum_convert_fusion.1, ...), kind=kLoop, calls=%fused_computation.277 | loop fusion | flops 19855616 | bytes 25767808 | tf_op jit(solution)/shard_map/reduce_sum | solution.py:162
  152.1 45.3 %while.29 = (s32[]{:T(128)}, bf16[6,128,4,64]{1,3,2,0:T(8,128)(2,1)S(1)}, f32[6,384,4,64]{1,3,2,0:T(8,128)}, f32[6,384,4,64]{1,3,2,0:T(8,128)S(1)}, bf16[6,384,4...) while((s32[]{:T(128)}, ...), condition=%wide.region_10.11_spmd.clone, body=%wide.region_9.10_spmd.clone.sunk | while | flops 127451136 | bytes 5426313 | solution.py:194
  152.9 1.3 fusion.237
  154.3 1.3 fusion.238
  155.6 1.2 fusion.239
  157.9 1.8 fusion.240
  160.5 1.3 fusion.237
  161.8 1.3 fusion.238
  163.1 1.2 fusion.239
  165.4 1.8 fusion.240
  168.0 1.3 fusion.237
  169.3 1.3 fusion.238
  172.9 1.8 fusion.240
  175.5 1.3 fusion.237
  176.9 1.3 fusion.238
  178.2 1.2 fusion.239
  180.5 1.8 fusion.240
  183.1 1.3 fusion.237
  184.4 1.3 fusion.238
  185.7 1.2 fusion.239
  188.0 1.8 fusion.240
  190.6 1.3 fusion.237
  192.0 1.3 fusion.238
  195.6 1.8 fusion.240
  197.4 2.0 fusion.48
  199.4 1.5 fusion.196
  200.9 2.5 collective-permute-start.6
  203.5 2.8 collective-permute-start.7
  207.4 113.5 %all-reduce.1 = (f32[1536]{0:T(1024)S(1)}, f32[1536]{0:T(1024)S(1)}) all-reduce(f32[1536]{0:T(1024)S(1)} %copy-done.39, f32[1536]{0:T(1024)S(1)} %copy-done.38), channel_id=1, replica_groups=mesh['dp'=8,'seq'=64] {'dp','seq'}, use_global_device_ids=true, to_apply=%region_12.13 | all-reduce | flops 3072 | bytes 24576 | tf_op jit(solution)/shard_map/psum | solution.py:216
  322.4 83.9 %all-reduce.4.cloned.1.call-done = f32[31,1536]{1,0:T(8,128)} async-done(((f32[31,1536]{1,0:T(8,128)}), f32[31,1536]{1,0:T(8,128)}) %all-reduce.4.cloned.1.call-update) | async-done | bytes 190480 | tf_op jit(solution)/shard_map/psum | solution.py:216
  406.3 1.6 broadcast_multiply_fusion
  407.9 1.9 fusion.52
  (231 shorter events, 54.3 us)
Async XLA Ops:
  7.2 21.0 %copy-start.2 = (bf16[1,128,1536]{2,1,0:T(8,128)(2,1)S(1)}, bf16[1,128,1536]{2,1,0:T(8,128)(2,1)}, u32[]{:S(2)}) copy-start(bf16[1,128,1536]{2,1,0:T(8,128)(2,1)} %param.14) | copy-start | bytes 1179652
  7.2 21.0 %copy-start.3 = (bf16[1,128,1536]{2,1,0:T(8,128)(2,1)S(1)}, bf16[1,128,1536]{2,1,0:T(8,128)(2,1)}, u32[]{:S(2)}) copy-start(bf16[1,128,1536]{2,1,0:T(8,128)(2,1)} %param.13) | copy-start | bytes 1179652
  7.2 15.3 %copy-start.4 = (bf16[1,128,1536]{2,1,0:T(8,128)(2,1)S(1)}, bf16[1,128,1536]{2,1,0:T(8,128)(2,1)}, u32[]{:S(2)}) copy-start(bf16[1,128,1536]{2,1,0:T(8,128)(2,1)} %param.12) | copy-start | bytes 1179652
  7.2 399.1 %all-reduce.4.cloned.1.call-start = ((), (), s32[]{:S(2)}) async-start(), calls=%async_computation | async-start | bytes 393216 | tf_op jit(solution)/shard_map/psum | solution.py:216
  8.5 17.8 %collective-permute-start.1 = (bf16[128,2,1536]{2,0,1:T(8,128)(2,1)S(1)}, bf16[128,2,1536]{2,0,1:T(8,128)(2,1)S(1)}, u32[]{:S(2)}, u32[]{:S(2)}) collective-permute-start(bf16[128,2,1536]{2,0,1:T(8,128)(2,1)S(1)} %pad_maximum_fusion.2), channel_id=1, source_target_pairs={{1,0},{2,1},{3,2},{4,3},{5,4},{6,5},{7,6},{8,7},{9,8},{10,9},{11,1... | collective-permute-start | bytes 2359304 | tf_op jit(solution)/shard_map/ppermute | solution.py:19
  17.3 10.8 %collective-permute-start = (bf16[128,2,1536]{2,0,1:T(8,128)(2,1)S(1)}, bf16[128,2,1536]{2,0,1:T(8,128)(2,1)S(1)}, u32[]{:S(2)}, u32[]{:S(2)}) collective-permute-start(bf16[128,2,1536]{2,0,1:T(8,128)(2,1)S(1)} %pad_maximum_fusion.2), channel_id=1, source_target_pairs={{0,1},{1,2},{2,3},{3,4},{4,5},{5,6},{6,7},{7,8},{8,9},{9,10},{10,1... | collective-permute-start | bytes 2359304 | tf_op jit(solution)/shard_map/ppermute | solution.py:19
  30.7 21.8 %copy-start.5 = (f32[1536]{0:T(1024)S(1)}, f32[1536]{0:T(1024)}, u32[]{:S(2)}) copy-start(f32[1536]{0:T(1024)} %param.16) | copy-start | bytes 18436
  52.3 8.1 %copy-start.57 = (f32[128]{0:T(128)}, f32[128]{0:T(128)S(1)}, u32[]{:S(2)}) copy-start(f32[128]{0:T(128)S(1)} %broadcast_multiply_fusion.5) | copy-start | bytes 1540
  52.5 7.8 %copy-start.59 = (f32[128]{0:T(128)}, f32[128]{0:T(128)S(1)}, u32[]{:S(2)}) copy-start(f32[128]{0:T(128)S(1)} %add_rsqrt_fusion) | copy-start | bytes 1540
  53.9 10.2 %collective-permute-start.2 = (bf16[15,1536]{0,1:T(8,128)(2,1)}, bf16[15,1536]{0,1:T(8,128)(2,1)}, u32[]{:S(2)}, u32[]{:S(2)}) collective-permute-start(bf16[15,1536]{0,1:T(8,128)(2,1)} %get-tuple-element.291), channel_id=1, source_target_pairs={{0,1},{1,2},{2,3},{3,4},{4,5},{5,6},{6,7},{7,8},{8,9},{9,10},{10,1... | collective-permute-start | bytes 138248 | tf_op jit(solution)/shard_map/ppermute | solution.py:30
  58.3 9.4 %collective-permute-start.3 = (bf16[15,1536]{0,1:T(8,128)(2,1)}, bf16[15,1536]{0,1:T(8,128)(2,1)}, u32[]{:S(2)}, u32[]{:S(2)}) collective-permute-start(bf16[15,1536]{0,1:T(8,128)(2,1)} %get-tuple-element.292), channel_id=1, source_target_pairs={{1,0},{2,1},{3,2},{4,3},{5,4},{6,5},{7,6},{8,7},{9,8},{10,9},{11,1... | collective-permute-start | bytes 138248 | tf_op jit(solution)/shard_map/ppermute | solution.py:32
  63.7 5.6 %copy-start.7 = (f32[1536]{0:T(1024)S(1)}, f32[1536]{0:T(1024)}, u32[]{:S(2)}) copy-start(f32[1536]{0:T(1024)} %get-tuple-element.199) | copy-start | bytes 18436
  63.7 5.6 %copy-start.8 = (f32[1536]{0:T(1024)S(1)}, f32[1536]{0:T(1024)}, u32[]{:S(2)}) copy-start(f32[1536]{0:T(1024)} %get-tuple-element.200) | copy-start | bytes 18436
  63.7 5.6 %copy-start.9 = (f32[1536]{0:T(1024)S(1)}, f32[1536]{0:T(1024)}, u32[]{:S(2)}) copy-start(f32[1536]{0:T(1024)} %get-tuple-element.201) | copy-start | bytes 18436
  63.7 5.6 %copy-start.10 = (f32[1536]{0:T(1024)S(1)}, f32[1536]{0:T(1024)}, u32[]{:S(2)}) copy-start(f32[1536]{0:T(1024)} %get-tuple-element.202) | copy-start | bytes 18436
  63.7 5.6 %copy-start.11 = (f32[1536]{0:T(1024)S(1)}, f32[1536]{0:T(1024)}, u32[]{:S(2)}) copy-start(f32[1536]{0:T(1024)} %get-tuple-element.203) | copy-start | bytes 18436
  63.7 5.6 %copy-start.12 = (f32[1536]{0:T(1024)S(1)}, f32[1536]{0:T(1024)}, u32[]{:S(2)}) copy-start(f32[1536]{0:T(1024)} %get-tuple-element.204) | copy-start | bytes 18436
  63.7 5.6 %copy-start.13 = (f32[1536]{0:T(1024)S(1)}, f32[1536]{0:T(1024)}, u32[]{:S(2)}) copy-start(f32[1536]{0:T(1024)} %get-tuple-element.205) | copy-start | bytes 18436
  63.8 5.6 %copy-start.14 = (f32[1536]{0:T(1024)S(1)}, f32[1536]{0:T(1024)}, u32[]{:S(2)}) copy-start(f32[1536]{0:T(1024)} %get-tuple-element.206) | copy-start | bytes 18436
  63.8 5.6 %copy-start.15 = (f32[1536]{0:T(1024)S(1)}, f32[1536]{0:T(1024)}, u32[]{:S(2)}) copy-start(f32[1536]{0:T(1024)} %get-tuple-element.207) | copy-start | bytes 18436
  63.8 5.6 %copy-start.16 = (f32[1536]{0:T(1024)S(1)}, f32[1536]{0:T(1024)}, u32[]{:S(2)}) copy-start(f32[1536]{0:T(1024)} %get-tuple-element.208) | copy-start | bytes 18436
  63.8 5.6 %copy-start.17 = (f32[1536]{0:T(1024)S(1)}, f32[1536]{0:T(1024)}, u32[]{:S(2)}) copy-start(f32[1536]{0:T(1024)} %get-tuple-element.209) | copy-start | bytes 18436
  63.8 5.6 %copy-start.18 = (f32[1536]{0:T(1024)S(1)}, f32[1536]{0:T(1024)}, u32[]{:S(2)}) copy-start(f32[1536]{0:T(1024)} %get-tuple-element.210) | copy-start | bytes 18436
  63.8 5.6 %copy-start.19 = (f32[1536]{0:T(1024)S(1)}, f32[1536]{0:T(1024)}, u32[]{:S(2)}) copy-start(f32[1536]{0:T(1024)} %get-tuple-element.211) | copy-start | bytes 18436
  63.8 5.6 %copy-start.20 = (f32[1536]{0:T(1024)S(1)}, f32[1536]{0:T(1024)}, u32[]{:S(2)}) copy-start(f32[1536]{0:T(1024)} %get-tuple-element.212) | copy-start | bytes 18436
  63.8 5.6 %copy-start.21 = (f32[1536]{0:T(1024)S(1)}, f32[1536]{0:T(1024)}, u32[]{:S(2)}) copy-start(f32[1536]{0:T(1024)} %get-tuple-element.213) | copy-start | bytes 18436
  63.8 5.6 %copy-start.22 = (f32[1536]{0:T(1024)S(1)}, f32[1536]{0:T(1024)}, u32[]{:S(2)}) copy-start(f32[1536]{0:T(1024)} %get-tuple-element.214) | copy-start | bytes 18436
  63.8 5.6 %copy-start.23 = (f32[1536]{0:T(1024)S(1)}, f32[1536]{0:T(1024)}, u32[]{:S(2)}) copy-start(f32[1536]{0:T(1024)} %get-tuple-element.215) | copy-start | bytes 18436
  63.9 5.6 %copy-start.24 = (f32[1536]{0:T(1024)S(1)}, f32[1536]{0:T(1024)}, u32[]{:S(2)}) copy-start(f32[1536]{0:T(1024)} %get-tuple-element.216) | copy-start | bytes 18436
  63.9 5.6 %copy-start.25 = (f32[1536]{0:T(1024)S(1)}, f32[1536]{0:T(1024)}, u32[]{:S(2)}) copy-start(f32[1536]{0:T(1024)} %get-tuple-element.217) | copy-start | bytes 18436
  63.9 5.6 %copy-start.26 = (f32[1536]{0:T(1024)S(1)}, f32[1536]{0:T(1024)}, u32[]{:S(2)}) copy-start(f32[1536]{0:T(1024)} %get-tuple-element.218) | copy-start | bytes 18436
  63.9 5.5 %copy-start.27 = (f32[1536]{0:T(1024)S(1)}, f32[1536]{0:T(1024)}, u32[]{:S(2)}) copy-start(f32[1536]{0:T(1024)} %get-tuple-element.219) | copy-start | bytes 18436
  63.9 5.5 %copy-start.28 = (f32[1536]{0:T(1024)S(1)}, f32[1536]{0:T(1024)}, u32[]{:S(2)}) copy-start(f32[1536]{0:T(1024)} %get-tuple-element.220) | copy-start | bytes 18436
  63.9 5.5 %copy-start.29 = (f32[1536]{0:T(1024)S(1)}, f32[1536]{0:T(1024)}, u32[]{:S(2)}) copy-start(f32[1536]{0:T(1024)} %get-tuple-element.221) | copy-start | bytes 18436
  63.9 5.5 %copy-start.30 = (f32[1536]{0:T(1024)S(1)}, f32[1536]{0:T(1024)}, u32[]{:S(2)}) copy-start(f32[1536]{0:T(1024)} %get-tuple-element.222) | copy-start | bytes 18436
  63.9 5.5 %copy-start.31 = (f32[1536]{0:T(1024)S(1)}, f32[1536]{0:T(1024)}, u32[]{:S(2)}) copy-start(f32[1536]{0:T(1024)} %get-tuple-element.223) | copy-start | bytes 18436
  63.9 5.5 %copy-start.32 = (f32[1536]{0:T(1024)S(1)}, f32[1536]{0:T(1024)}, u32[]{:S(2)}) copy-start(f32[1536]{0:T(1024)} %get-tuple-element.224) | copy-start | bytes 18436
  64.0 5.5 %copy-start.33 = (f32[1536]{0:T(1024)S(1)}, f32[1536]{0:T(1024)}, u32[]{:S(2)}) copy-start(f32[1536]{0:T(1024)} %get-tuple-element.225) | copy-start | bytes 18436
  64.0 5.5 %copy-start.34 = (f32[1536]{0:T(1024)S(1)}, f32[1536]{0:T(1024)}, u32[]{:S(2)}) copy-start(f32[1536]{0:T(1024)} %get-tuple-element.226) | copy-start | bytes 18436
  64.0 5.5 %copy-start.35 = (f32[1536]{0:T(1024)S(1)}, f32[1536]{0:T(1024)}, u32[]{:S(2)}) copy-start(f32[1536]{0:T(1024)} %get-tuple-element.227) | copy-start | bytes 18436
  64.0 5.5 %copy-start.36 = (f32[1536]{0:T(1024)S(1)}, f32[1536]{0:T(1024)}, u32[]{:S(2)}) copy-start(f32[1536]{0:T(1024)} %get-tuple-element.228) | copy-start | bytes 18436
  64.0 5.5 %copy-start.37 = (f32[1536]{0:T(1024)S(1)}, f32[1536]{0:T(1024)}, u32[]{:S(2)}) copy-start(f32[1536]{0:T(1024)} %get-tuple-element.229) | copy-start | bytes 18436
  64.0 5.5 %copy-start.40 = (pred[128]{0:T(512)(128)(4,1)S(1)}, pred[128]{0:T(512)(128)(4,1)}, u32[]{:S(2)}) copy-start(pred[128]{0:T(512)(128)(4,1)} %get-tuple-element.311) | copy-start | bytes 388
  64.0 5.5 %copy-start.41 = (pred[128]{0:T(512)(128)(4,1)S(1)}, pred[128]{0:T(512)(128)(4,1)}, u32[]{:S(2)}) copy-start(pred[128]{0:T(512)(128)(4,1)} %get-tuple-element.312) | copy-start | bytes 388
  64.0 5.5 %copy-start.42 = (pred[128]{0:T(512)(128)(4,1)S(1)}, pred[128]{0:T(512)(128)(4,1)}, u32[]{:S(2)}) copy-start(pred[128]{0:T(512)(128)(4,1)} %get-tuple-element.313) | copy-start | bytes 388
  64.0 5.5 %copy-start.43 = (pred[128]{0:T(512)(128)(4,1)S(1)}, pred[128]{0:T(512)(128)(4,1)}, u32[]{:S(2)}) copy-start(pred[128]{0:T(512)(128)(4,1)} %get-tuple-element.314) | copy-start | bytes 388
  64.0 5.5 %copy-start.44 = (pred[128]{0:T(512)(128)(4,1)S(1)}, pred[128]{0:T(512)(128)(4,1)}, u32[]{:S(2)}) copy-start(pred[128]{0:T(512)(128)(4,1)} %get-tuple-element.315) | copy-start | bytes 388
  64.1 5.5 %copy-start.45 = (pred[128]{0:T(512)(128)(4,1)S(1)}, pred[128]{0:T(512)(128)(4,1)}, u32[]{:S(2)}) copy-start(pred[128]{0:T(512)(128)(4,1)} %get-tuple-element.316) | copy-start | bytes 388
  64.1 5.5 %copy-start.46 = (pred[128]{0:T(512)(128)(4,1)S(1)}, pred[128]{0:T(512)(128)(4,1)}, u32[]{:S(2)}) copy-start(pred[128]{0:T(512)(128)(4,1)} %get-tuple-element.317) | copy-start | bytes 388
  64.1 5.5 %copy-start.47 = (pred[128]{0:T(512)(128)(4,1)S(1)}, pred[128]{0:T(512)(128)(4,1)}, u32[]{:S(2)}) copy-start(pred[128]{0:T(512)(128)(4,1)} %get-tuple-element.318) | copy-start | bytes 388
  64.1 5.5 %copy-start.48 = (pred[128]{0:T(512)(128)(4,1)S(1)}, pred[128]{0:T(512)(128)(4,1)}, u32[]{:S(2)}) copy-start(pred[128]{0:T(512)(128)(4,1)} %get-tuple-element.319) | copy-start | bytes 388
  96.6 6.2 %copy-start.54 = (pred[128]{0:T(512)(128)(4,1)S(1)}, pred[128]{0:T(512)(128)(4,1)}, u32[]{:S(2)}) copy-start(pred[128]{0:T(512)(128)(4,1)} %get-tuple-element.297) | copy-start | bytes 388
  96.6 6.2 %copy-start.55 = (pred[128]{0:T(512)(128)(4,1)S(1)}, pred[128]{0:T(512)(128)(4,1)}, u32[]{:S(2)}) copy-start(pred[128]{0:T(512)(128)(4,1)} %get-tuple-element.298) | copy-start | bytes 388
  96.6 6.2 %copy-start.56 = (pred[128]{0:T(512)(128)(4,1)S(1)}, pred[128]{0:T(512)(128)(4,1)}, u32[]{:S(2)}) copy-start(pred[128]{0:T(512)(128)(4,1)} %get-tuple-element.299) | copy-start | bytes 388
  97.5 32.0 %collective-permute-start.4 = (bf16[15,1536]{0,1:T(8,128)(2,1)}, bf16[15,1536]{0,1:T(8,128)(2,1)}, u32[]{:S(2)}, u32[]{:S(2)}) collective-permute-start(bf16[15,1536]{0,1:T(8,128)(2,1)} %get-tuple-element.289), channel_id=1, source_target_pairs={{0,1},{1,2},{2,3},{3,4},{4,5},{5,6},{6,7},{7,8},{8,9},{9,10},{10,1... | collective-permute-start | bytes 138248 | tf_op jit(solution)/shard_map/ppermute | solution.py:30
  99.4 30.1 %collective-permute-start.5 = (bf16[15,1536]{0,1:T(8,128)(2,1)S(1)}, bf16[15,1536]{0,1:T(8,128)(2,1)}, u32[]{:S(2)}, u32[]{:S(2)}) collective-permute-start(bf16[15,1536]{0,1:T(8,128)(2,1)S(1)} %get-tuple-element.290), channel_id=1, source_target_pairs={{1,0},{2,1},{3,2},{4,3},{5,4},{6,5},{7,6},{8,7},{9,8},{10,9},{11,1... | collective-permute-start | bytes 138248 | tf_op jit(solution)/shard_map/ppermute | solution.py:32
  131.1 19.2 %copy-start.6 = (f32[1536]{0:T(1024)S(1)}, f32[1536]{0:T(1024)}, u32[]{:S(2)}) copy-start(f32[1536]{0:T(1024)} %param.16) | copy-start | bytes 18436
  131.1 19.2 %copy-start.58 = (f32[128]{0:T(128)S(1)}, f32[128]{0:T(128)}, u32[]{:S(2)}) copy-start(f32[128]{0:T(128)} %copy-done.57) | copy-start | bytes 1540
  131.1 19.2 %copy-start.60 = (f32[128]{0:T(128)S(1)}, f32[128]{0:T(128)}, u32[]{:S(2)}) copy-start(f32[128]{0:T(128)} %copy-done.59) | copy-start | bytes 1540
  199.4 6.8 %copy-start.1 = (f32[128,1536]{0,1:T(8,128)S(1)}, f32[128,1536]{0,1:T(8,128)}, u32[]{:S(2)}) copy-start(f32[128,1536]{0,1:T(8,128)} %get-tuple-element.273) | copy-start | bytes 2359300
  200.9 6.5 %copy-start.38 = (f32[1536]{0:T(1024)S(1)}, f32[1536]{0:T(1024)}, u32[]{:S(2)}) copy-start(f32[1536]{0:T(1024)} %get-tuple-element.198) | copy-start | bytes 18436
  200.9 6.5 %copy-start.39 = (f32[1536]{0:T(1024)S(1)}, f32[1536]{0:T(1024)}, u32[]{:S(2)}) copy-start(f32[1536]{0:T(1024)} %get-tuple-element.195) | copy-start | bytes 18436
  200.9 207.0 %collective-permute-start.6 = (bf16[128,2,1536]{0,2,1:T(8,128)(2,1)}, bf16[128,2,1536]{0,2,1:T(8,128)(2,1)}, u32[]{:S(2)}, u32[]{:S(2)}) collective-permute-start(bf16[128,2,1536]{0,2,1:T(8,128)(2,1)} %get-tuple-element.283), channel_id=1, source_target_pairs={{0,1},{1,2},{2,3},{3,4},{4,5},{5,6},{6,7},{7,8},{8,9},{9,10},{10,1... | collective-permute-start | bytes 2359304 | tf_op jit(solution)/shard_map/ppermute | solution.py:19
  203.5 204.5 %collective-permute-start.7 = (bf16[128,2,1536]{0,2,1:T(8,128)(2,1)}, bf16[128,2,1536]{0,2,1:T(8,128)(2,1)}, u32[]{:S(2)}, u32[]{:S(2)}) collective-permute-start(bf16[128,2,1536]{0,2,1:T(8,128)(2,1)} %get-tuple-element.284), channel_id=1, source_target_pairs={{1,0},{2,1},{3,2},{4,3},{5,4},{6,5},{7,6},{8,7},{9,8},{10,9},{11,1... | collective-permute-start | bytes 2359304 | tf_op jit(solution)/shard_map/ppermute | solution.py:19
  (6 other events, 24.2 us)
Sparse Core Ops, SparseCore 0:
  129.6 276.6 all-reduce.3
where the time goes:
time: 421 us; the launch traced here: 419 us
  blocking collectives  113 us (27%)
  waiting for transfers between devices  89.3 us (21%)
  other arithmetic  70.2 us (17%)
  matrix products  55.7 us (13%)
  local copies, waits for them, and re-layouts  46.8 us (11%)
  starting transfers between devices  27.8 us (7%)
  between operations  15.1 us (4%)
    psum x1, blocking collectives, per_device(): lax.psum((gain_part, kernel_part, bias_part), ('dp', 'seq'))  113 us
    psum x1, waiting for transfers between devices, per_device(): lax.psum((gain_part, kernel_part, bias_part), ('dp', 'seq'))  83.9 us
    reduce_sum x4, other arithmetic, per_device(): jnp.sum(jnp.where(same_taps[tap_index], conv_wide[tap_index:tap_index + f...  29 us
    another operation x32, local copies, waits for them, and re-layouts, per_device(): kernel_part = jnp.stack(kernel_rows, 0)  24.4 us
    reduce_sum x1, other arithmetic, per_device(): gain_part = jnp.sum(grad_in * normed, 0)  19.2 us
    ppermute x4, starting transfers between devices, shifted(): return lax.ppermute(block, axis, route)  16 us
    dot_general x12, matrix products, masked_logits(): jnp.einsum('qhe,khe->hqk', query_rows, key_rows, preferred_element_type=j...  15.4 us
    dot_general x6, matrix products, backward_group(): jnp.einsum('hqk,qhe->khe', grad_logit, query_rows, preferred_element_type...  10.9 us
  transfers between devices with their start and end apart: 9, of which 3 were waited for; matrix products, arithmetic and copies ran while one was open for 27% of the time, Pallas kernels for 0%

commit v1 on v0

v1 whole, which is shorter than its diff:
```python
import functools

import jax
import jax.numpy as jnp
from jax import lax
from jax.experimental import pallas as pl
from jax.experimental.pallas import tpu as pltpu
from jax.sharding import PartitionSpec as P

BF = jnp.bfloat16
F32 = jnp.float32
HEADS = 24
HEAD_DIM = 64
TAPS = 31
FR = 128
WIDE = 384
LANES = 128
PAIRS = HEADS * HEAD_DIM // LANES
WIDTH = HEADS * HEAD_DIM
EPS = 1e-05
NEG = -1e30
LOG2E = 1.4426950408889634
SCALE = HEAD_DIM ** (-0.5)
NX = 4
NC = 2
TILES = PAIRS * 4
HALF_TILES = TILES // NC
PIECE = HALF_TILES // NX
MESH = pl.DeviceIdType.MESH


def lanes_of(p):
    return pl.ds(pl.multiple_of(p * LANES, LANES), LANES)


def dot_nt(a, b):
    return lax.dot_general(a, b, (((1,), (1,)), ((), ())), preferred_element_type=F32)


def dot_nn(a, b):
    return lax.dot_general(a, b, (((1,), (0,)), ((), ())), preferred_element_type=F32)


def kernel(
    nz,
    ny,
    q_hbm,
    k_hbm,
    v_hbm,
    cot_hbm,
    seg_hbm,
    gain_ref,
    ker_ref,
    bias_ref,
    conv_hbm,
    dq_hbm,
    dk_hbm,
    dv_hbm,
    gain_out,
    ker_out,
    bias_out,
    kbuf,
    vbuf,
    qbuf,
    cotbuf,
    segbuf,
    segc,
    maskb,
    cm,
    wb,
    bb,
    gb,
    pbuf,
    ctx,
    ctxt,
    xbuf,
    gbuf,
    meanb,
    invb,
    acc1,
    acc2,
    xsend,
    xrecv,
    gsend,
    grecv,
    kg,
    dkv_own,
    dkv_send,
    dkv_recv,
    dq_buf,
    conv_buf,
    red,
    core_in,
    half,
    xg,
    other_in,
    tot,
    x_in,
    z_in,
    y_in,
    lsem,
    osem,
    kv_s,
    kv_r,
    xs,
    xr,
    gs,
    gr,
    d_s,
    d_r,
    c_s,
    c_r,
    x_s,
    x_r,
    z_s,
    z_r,
    y_s,
    y_r,
    ax_s,
    ax_r,
    ac_s,
    ac_r,
):
    nseq = nz * NX * NC
    me = lax.axis_index("seq")
    row = lax.axis_index("dp")
    right = lax.rem(me + 1, nseq)
    left = lax.rem(me + nseq - 1, nseq)
    core = lax.rem(me, NC)
    mx = lax.rem(me // NC, NX)
    mz = me // (NC * NX)

    def seq_dev(s):
        return (row, s)

    def x_dev(k):
        return seq_dev(mz * (NC * NX) + lax.rem(mx + k, NX) * NC + core)

    def z_dev(k):
        return seq_dev(lax.rem(mz + k, nz) * (NC * NX) + lax.rem(me, NC * NX))

    def y_dev(k):
        return (lax.rem(row + k, ny), me)

    core_dev = seq_dev(me + 1 - 2 * core)
    sides = (seq_dev(right), seq_dev(left))

    def remote(src, dst, s, r, dev):
        return pltpu.make_async_remote_copy(
            src_ref=src, dst_ref=dst, send_sem=s, recv_sem=r, device_id=dev, device_id_type=MESH
        )

    own = pl.ds(FR, FR)
    locals_ = [
        pltpu.make_async_copy(k_hbm, kbuf.at[own, :], lsem.at[0]),
        pltpu.make_async_copy(v_hbm, vbuf.at[own, :], lsem.at[1]),
        pltpu.make_async_copy(q_hbm, qbuf, lsem.at[2]),
        pltpu.make_async_copy(cot_hbm, cotbuf, lsem.at[3]),
    ]
    for j, blk in enumerate((left, me, right)):
        locals_.append(
            pltpu.make_async_copy(
                seg_hbm.at[:, pl.ds(pl.multiple_of(blk * FR, FR), FR)],
                segbuf.at[j],
                lsem.at[4 + j],
            )
        )
    for copy in locals_[::-1]:
        copy.start()

    barrier = pltpu.get_barrier_semaphore()
    partners = list(sides)
    partners += [x_dev(k) for k in range(1, NX)]
    partners += [z_dev(k) for k in range(1, nz)]
    partners += [y_dev(k) for k in range(1, ny)]
    for dev in partners:
        pl.semaphore_signal(barrier, inc=1, device_id=dev, device_id_type=MESH)
    pl.semaphore_wait(barrier, len(partners))

    def kv_copy(side, kv, p):
        src = (k_hbm, v_hbm)[kv]
        dst = (kbuf, vbuf)[kv]
        at = 0 if side == 0 else 2 * FR
        return remote(
            src.at[:, lanes_of(p)],
            dst.at[pl.ds(at, FR), lanes_of(p)],
            kv_s.at[side, kv, p],
            kv_r.at[side, kv, p],
            sides[side],
        )

    @pl.loop(0, PAIRS)
    def _(p):
        for kv in range(2):
            for side in range(2):
                kv_copy(side, kv, p).start()

    for j in range(3):
        locals_[4 + j].wait()
    own_row = segbuf[1]
    for j in range(3):
        col = jnp.broadcast_to(segbuf[j], (FR, LANES)).T
        segc[pl.ds(j * FR, FR), :] = col
        maskb[pl.ds(j * FR, FR), :] = jnp.where(col == own_row, 0.0, NEG)
    own_col = segc[pl.ds(FR, FR), :]
    for t in range(TAPS):
        cm[t] = jnp.where(segc[pl.ds(FR + t - 15, FR), :] == own_col, 1.0, 0.0)

    @pl.loop(0, PAIRS)
    def _(c):
        for t in range(TAPS):
            wb[c, t] = jnp.broadcast_to(ker_ref[t : t + 1, lanes_of(c)], (8, LANES))
        bb[c] = jnp.broadcast_to(bias_ref[:, lanes_of(c)], (8, LANES))
        gb[c] = jnp.broadcast_to(gain_ref[:, lanes_of(c)], (8, LANES))
        kg[c] = jnp.zeros_like(kg[c])

    for j in range(3):
        locals_[j].wait()
    low = lax.broadcasted_iota(jnp.int32, (FR, LANES), 1) < HEAD_DIM

    def diag(block):
        zero = jnp.zeros_like(block)
        return jnp.concatenate([jnp.where(low, block, zero), jnp.where(low, zero, block)], 0)

    def pick(block):
        return jnp.concatenate([block[:HEAD_DIM, :LANES], block[HEAD_DIM:, LANES:]], 0)

    @pl.loop(0, PAIRS)
    def _(p):
        for kv in range(2):
            for side in range(2):
                kv_copy(side, kv, p).wait_recv()
        key = kbuf[:, lanes_of(p)]
        val = vbuf[:, lanes_of(p)]
        qd = diag(qbuf[:, lanes_of(p)])
        mask = maskb[...]
        s = dot_nt(key, qd) * (SCALE * LOG2E) + jnp.concatenate([mask, mask], 1)
        top = jnp.max(s, 0, keepdims=True)
        e = jnp.exp2(s - top)
        inv = 1.0 / jnp.sum(e, 0, keepdims=True)
        prob = (e * inv).astype(BF)
        pbuf[p] = prob
        ct = pick(dot_nn(val.T, prob)).astype(BF).astype(F32)
        ctxt[p] = ct
        ctx[p] = ct.T

    zero = jnp.zeros((FR, LANES), F32)
    total = lax.fori_loop(0, PAIRS, lambda c, a: a + ctx[c], zero)
    mean = jnp.broadcast_to(jnp.sum(total, 1, keepdims=True) * (1.0 / WIDTH), (FR, LANES))
    meanb[...] = mean

    def square(c, a):
        d = ctx[c] - meanb[...]
        return a + d * d

    total = lax.fori_loop(0, PAIRS, square, zero)
    var = jnp.sum(total, 1, keepdims=True) * (1.0 / WIDTH)
    invb[...] = jnp.broadcast_to(lax.rsqrt(var + EPS), (FR, LANES))

    @pl.loop(0, PAIRS)
    def _(c):
        normed = (ctx[c] - meanb[...]) * invb[...]
        ctx[c] = normed
        x = (normed.reshape(16, 8, LANES) * gb[c][None]).reshape(FR, LANES).astype(BF)
        xsend[1, c] = x[:16]
        xsend[0, c] = x[FR - 16 :]
        xbuf[c, pl.ds(16, FR), :] = x.astype(F32)

    def x_copy(side):
        return remote(xsend.at[side], xrecv.at[side], xs.at[side], xr.at[side], sides[side])

    def g_copy(side):
        return remote(gsend.at[side], grecv.at[side], gs.at[side], gr.at[side], sides[side])

    for side in range(2):
        x_copy(side).start()
    locals_[3].wait()

    def conv_group(chunks, tiles):
        acc = [[bb[c] for _ in tiles] for c in chunks]
        for t in range(TAPS):
            ms = [cm[t, pl.ds(r, 8), :] for r in tiles]
            for j, c in enumerate(chunks):
                w = wb[c, t]
                for i, r in enumerate(tiles):
                    acc[j][i] = acc[j][i] + w * (ms[i] * xbuf[c, pl.ds(r + t + 1, 8), :])
        gr_ = []
        for j, c in enumerate(chunks):
            gr_.append([])
            for i, r in enumerate(tiles):
                a = acc[j][i]
                sig = 1.0 / (1.0 + jnp.exp(-a))
                acc[j][i] = a * sig
                gr_[j].append(sig * (1.0 + a * (1.0 - sig)))
        bias_sum = []
        for j, c in enumerate(chunks):
            for h in range(0, len(tiles), 2):
                r = tiles[h]
                out = jnp.concatenate(acc[j][h : h + 2], 0).astype(BF)
                conv_buf[pl.ds(r, 16), lanes_of(c)] = out
                g = jnp.concatenate(gr_[j][h : h + 2], 0)
                g = (g * cotbuf[pl.ds(r, 16), lanes_of(c)].astype(F32)).astype(BF)
                if isinstance(r, int) and r == 0:
                    gsend[1, c] = g
                elif isinstance(r, int) and r == FR - 16:
                    gsend[0, c] = g
                g = g.astype(F32)
                gbuf[c, pl.ds(r + 16, 16), :] = g
                gr_[j][h] = g[:8]
                gr_[j][h + 1] = g[8:]
            kg[c, TAPS] = kg[c, TAPS] + functools.reduce(jnp.add, gr_[j])
        for t in range(TAPS):
            ms = [cm[t, pl.ds(r, 8), :] for r in tiles]
            for j, c in enumerate(chunks):
                terms = [
                    gr_[j][i] * (ms[i] * xbuf[c, pl.ds(r + t + 1, 8), :])
                    for i, r in enumerate(tiles)
                ]
                kg[c, t] = kg[c, t] + functools.reduce(jnp.add, terms)

    edges = [0, 8, FR - 16, FR - 8]

    @pl.loop(0, PAIRS // 2)
    def _(cc):
        @pl.loop(0, 3)
        def _(rr):
            r0 = pl.multiple_of(rr * 32 + 16, 16)
            conv_group([2 * cc, 2 * cc + 1], [pl.multiple_of(r0 + 8 * i, 8) for i in range(4)])

    for side in range(2):
        x_copy(side).wait_recv()

    @pl.loop(0, PAIRS // 2)
    def _(cc):
        for c in (2 * cc, 2 * cc + 1):
            xbuf[c, pl.ds(0, 16), :] = xrecv[0, c].astype(F32)
            xbuf[c, pl.ds(FR + 16, 16), :] = xrecv[1, c].astype(F32)
        conv_group([2 * cc, 2 * cc + 1], edges)

    for side in range(2):
        g_copy(side).start()

    @pl.loop(0, PAIRS)
    def _(c):
        for rg in range(4):
            red[rg * PAIRS + c] = jnp.sum(kg[c, pl.ds(rg * 8, 8)], 1)

    conv_done = pltpu.make_async_copy(conv_buf, conv_hbm, osem.at[0])
    conv_done.start()

    other = (1 - core) * HALF_TILES
    mine = core * HALF_TILES
    core_copy = remote(red.at[pl.ds(other, HALF_TILES)], core_in, c_s, c_r, core_dev)
    core_copy.start()

    def in_group(chunks, tiles):
        acc = [[None for _ in tiles] for c in chunks]
        for u in range(TAPS):
            ms = [cm[u, pl.ds(r, 8), :] for r in tiles]
            for j, c in enumerate(chunks):
                w = wb[c, TAPS - 1 - u]
                for i, r in enumerate(tiles):
                    term = w * (ms[i] * gbuf[c, pl.ds(r + u + 1, 8), :])
                    acc[j][i] = term if u == 0 else acc[j][i] + term
        for i, r in enumerate(tiles):
            s1 = acc1[pl.ds(r, 8), :]
            s2 = acc2[pl.ds(r, 8), :]
            for j, c in enumerate(chunks):
                g = acc[j][i] * gb[c]
                dkv_own[0, c, pl.ds(r, 8), :] = g
                s1 = s1 + g
                s2 = s2 + g * ctx[c, pl.ds(r, 8), :]
            acc1[pl.ds(r, 8), :] = s1
            acc2[pl.ds(r, 8), :] = s2

    acc1[...] = zero
    acc2[...] = zero

    @pl.loop(0, PAIRS // 2)
    def _(cc):
        @pl.loop(0, 3)
        def _(rr):
            r0 = pl.multiple_of(rr * 32 + 16, 16)
            in_group([2 * cc, 2 * cc + 1], [pl.multiple_of(r0 + 8 * i, 8) for i in range(4)])

    core_copy.wait_recv()

    @pl.loop(0, HALF_TILES)
    def _(i):
        half[i] = red[mine + i] + core_in[i]

    def x_red(k):
        to = lax.rem(mx + k, NX)
        return remote(
            half.at[pl.ds(to * PIECE, PIECE)], x_in.at[mx], x_s.at[k - 1], x_r.at[k - 1], x_dev(k)
        )

    for k in range(1, NX):
        x_red(k).start()
    x_in[mx] = half[pl.ds(mx * PIECE, PIECE)]

    for side in range(2):
        g_copy(side).wait_recv()

    @pl.loop(0, PAIRS // 2)
    def _(cc):
        for c in (2 * cc, 2 * cc + 1):
            gbuf[c, pl.ds(0, 16), :] = grecv[0, c].astype(F32)
            gbuf[c, pl.ds(FR + 16, 16), :] = grecv[1, c].astype(F32)
        in_group([2 * cc, 2 * cc + 1], edges)

    acc1[...] = jnp.broadcast_to(jnp.sum(acc1[...], 1, keepdims=True) * (1.0 / WIDTH), (FR, LANES))
    acc2[...] = jnp.broadcast_to(jnp.sum(acc2[...], 1, keepdims=True) * (1.0 / WIDTH), (FR, LANES))

    def d_copy(side, kv, p):
        return remote(
            dkv_send.at[side, kv, :, lanes_of(p)],
            dkv_recv.at[side, kv, :, lanes_of(p)],
            d_s.at[side, kv, p],
            d_r.at[side, kv, p],
            sides[side],
        )

    def back(p):
        dc = (dkv_own[0, p] - acc1[...] - ctx[p] * acc2[...]) * invb[...]
        dc = dc.astype(BF)
        prod = dc.astype(F32).T * ctxt[p]
        delta = jnp.concatenate(
            [
                jnp.sum(prod[:HEAD_DIM], 0, keepdims=True),
                jnp.sum(prod[HEAD_DIM:], 0, keepdims=True),
            ],
            1,
        )
        key = kbuf[:, lanes_of(p)]
        val = vbuf[:, lanes_of(p)]
        dcd = diag(dc)
        qd = diag(qbuf[:, lanes_of(p)])
        prob = pbuf[p]
        dp = dot_nt(val, dcd)
        ds = (prob.astype(F32) * ((dp - delta) * SCALE)).astype(BF)
        dv = dot_nn(prob, dcd)
        dk = dot_nn(ds, qd)
        dq = pick(dot_nn(key.T, ds)).T
        dq_buf[:, lanes_of(p)] = dq.astype(BF)
        for kv, d in enumerate((dk, dv)):
            dkv_send[1, kv, :, lanes_of(p)] = d[:FR].astype(BF)
            dkv_own[kv, p] = d[FR : 2 * FR]
            dkv_send[0, kv, :, lanes_of(p)] = d[2 * FR :].astype(BF)
        for kv in range(2):
            for side in range(2):
                d_copy(side, kv, p).start()

    pl.loop(0, 3)(back)

    for k in range(1, NX):
        x_red(k).wait_recv()
    z_in[mz] = (x_in[0] + x_in[1]) + (x_in[2] + x_in[3])

    def z_copy(k):
        return remote(z_in.at[mz], z_in.at[mz], z_s.at[k - 1], z_r.at[k - 1], z_dev(k))

    def y_copy(k):
        return remote(y_in.at[row], y_in.at[row], y_s.at[k - 1], y_r.at[k - 1], y_dev(k))

    far_z = sorted(range(1, nz), key=lambda k: -min(k, nz - k))
    far_y = sorted(range(1, ny), key=lambda k: -min(k, ny - k))
    for k in far_z:
        z_copy(k).start()

    pl.loop(3, 8)(back)

    for k in far_z:
        z_copy(k).wait_recv()
    y_in[row] = functools.reduce(jnp.add, [z_in[i] for i in range(nz)])
    for k in far_y:
        y_copy(k).start()

    pl.loop(8, PAIRS)(back)

    dq_done = pltpu.make_async_copy(dq_buf, dq_hbm, osem.at[1])
    dq_done.start()

    for k in far_y:
        y_copy(k).wait_recv()
    xg[pl.ds(mx * PIECE, PIECE)] = functools.reduce(jnp.add, [y_in[i] for i in range(ny)])

    def x_gather(k):
        here = pl.ds(mx * PIECE, PIECE)
        return remote(xg.at[here], xg.at[here], ax_s.at[k - 1], ax_r.at[k - 1], x_dev(k))

    for k in range(1, NX):
        x_gather(k).start()

    @pl.loop(0, PAIRS)
    def _(p):
        for kv in range(2):
            for side in range(2):
                d_copy(side, kv, p).wait_recv()
            d = dkv_own[kv, p]
            d = d + dkv_recv[0, kv, :, lanes_of(p)].astype(F32)
            d = d + dkv_recv[1, kv, :, lanes_of(p)].astype(F32)
            (kbuf, vbuf)[kv][pl.ds(FR, FR), lanes_of(p)] = d.astype(BF)

    dk_done = pltpu.make_async_copy(kbuf.at[own, :], dk_hbm, osem.at[2])
    dv_done = pltpu.make_async_copy(vbuf.at[own, :], dv_hbm, osem.at[3])
    dk_done.start()
    dv_done.start()

    for k in range(1, NX):
        x_gather(k).wait_recv()
    gather_copy = remote(xg, other_in, ac_s, ac_r, core_dev)
    gather_copy.start()
    gather_copy.wait_recv()
    factor = (ny * nseq * FR) ** (-0.5)

    @pl.loop(0, HALF_TILES)
    def _(i):
        tot[mine + i] = xg[i]
        tot[other + i] = other_in[i]

    for c in range(PAIRS):
        at = slice(c * LANES, (c + 1) * LANES)
        gsum = jnp.zeros((8, LANES), F32)
        for rg in range(4):
            tile = tot[rg * PAIRS + c] * factor
            if rg < 3:
                ker_out[rg * 8 : rg * 8 + 8, at] = tile
                gsum = gsum + tile * ker_ref[rg * 8 : rg * 8 + 8, at]
            else:
                ker_out[24:31, at] = tile[:7]
                bias_out[:, at] = tile[7:]
                gsum = gsum + jnp.concatenate(
                    [tile[:7] * ker_ref[24:31, at], jnp.zeros((1, LANES), F32)], 0
                )
        gain_out[:, at] = jnp.sum(gsum, 0, keepdims=True) / gain_ref[:, at]

    @pl.loop(0, PAIRS)
    def _(p):
        for kv in range(2):
            for side in range(2):
                kv_copy(side, kv, p).wait_send()
                d_copy(side, kv, p).wait_send()

    for side in range(2):
        x_copy(side).wait_send()
        g_copy(side).wait_send()
    for k in range(1, NX):
        x_red(k).wait_send()
        x_gather(k).wait_send()
    for k in far_z:
        z_copy(k).wait_send()
    for k in far_y:
        y_copy(k).wait_send()
    core_copy.wait_send()
    gather_copy.wait_send()
    conv_done.wait()
    dq_done.wait()
    dk_done.wait()
    dv_done.wait()


def per_device(nz, ny, queries, keys, values, segment_ids, norm_gain, conv_kernel, conv_bias, cot):
    dma = pltpu.SemaphoreType.DMA
    vmem = pltpu.VMEM
    any_ = pl.BlockSpec(memory_space=pl.ANY)
    whole = pl.BlockSpec(memory_space=pltpu.VMEM)
    row = jax.ShapeDtypeStruct((FR, WIDTH), BF)
    outs = pl.pallas_call(
        functools.partial(kernel, nz, ny),
        out_shape=(
            row,
            row,
            row,
            row,
            jax.ShapeDtypeStruct((1, WIDTH), F32),
            jax.ShapeDtypeStruct((TAPS, WIDTH), F32),
            jax.ShapeDtypeStruct((1, WIDTH), F32),
        ),
        in_specs=[any_] * 5 + [whole] * 3,
        out_specs=(any_, any_, any_, any_, whole, whole, whole),
        scratch_shapes=[
            vmem((WIDE, WIDTH), BF),
            vmem((WIDE, WIDTH), BF),
            vmem((FR, WIDTH), BF),
            vmem((FR, WIDTH), BF),
            vmem((3, 1, FR), jnp.int32),
            vmem((WIDE, LANES), jnp.int32),
            vmem((WIDE, LANES), F32),
            vmem((TAPS, FR, LANES), F32),
            vmem((PAIRS, TAPS, 8, LANES), F32),
            vmem((PAIRS, 8, LANES), F32),
            vmem((PAIRS, 8, LANES), F32),
            vmem((PAIRS, WIDE, 2 * LANES), BF),
            vmem((PAIRS, FR, LANES), F32),
            vmem((PAIRS, FR, LANES), F32),
            vmem((PAIRS, FR + 32, LANES), F32),
            vmem((PAIRS, FR + 32, LANES), F32),
            vmem((FR, LANES), F32),
            vmem((FR, LANES), F32),
            vmem((FR, LANES), F32),
            vmem((FR, LANES), F32),
            vmem((2, PAIRS, 16, LANES), BF),
            vmem((2, PAIRS, 16, LANES), BF),
            vmem((2, PAIRS, 16, LANES), BF),
            vmem((2, PAIRS, 16, LANES), BF),
            vmem((PAIRS, 32, 8, LANES), F32),
            vmem((2, PAIRS, FR, LANES), F32),
            vmem((2, 2, FR, WIDTH), BF),
            vmem((2, 2, FR, WIDTH), BF),
            vmem((FR, WIDTH), BF),
            vmem((FR, WIDTH), BF),
            vmem((TILES, 8, LANES), F32),
            vmem((HALF_TILES, 8, LANES), F32),
            vmem((HALF_TILES, 8, LANES), F32),
            vmem((HALF_TILES, 8, LANES), F32),
            vmem((HALF_TILES, 8, LANES), F32),
            vmem((TILES, 8, LANES), F32),
            vmem((NX, PIECE, 8, LANES), F32),
            vmem((nz, PIECE, 8, LANES), F32),
            vmem((ny, PIECE, 8, LANES), F32),
            dma((7,)),
            dma((4,)),
            dma((2, 2, PAIRS)),
            dma((2, 2, PAIRS)),
            dma((2,)),
            dma((2,)),
            dma((2,)),
            dma((2,)),
            dma((2, 2, PAIRS)),
            dma((2, 2, PAIRS)),
            dma,
            dma,
            dma((NX - 1,)),
            dma((NX - 1,)),
            dma((nz - 1,)),
            dma((nz - 1,)),
            dma((ny - 1,)),
            dma((ny - 1,)),
            dma((NX - 1,)),
            dma((NX - 1,)),
            dma,
            dma,
        ],
        compiler_params=pltpu.CompilerParams(
            collective_id=0, has_side_effects=True, vmem_limit_bytes=56 * 1024 * 1024
        ),
    )(
        queries[0],
        keys[0],
        values[0],
        cot[0],
        segment_ids,
        norm_gain.reshape(1, WIDTH),
        conv_kernel,
        conv_bias.reshape(1, WIDTH),
    )
    conv_out, dq, dk, dv, gain, ker, bias = outs
    return (
        conv_out[None],
        dq[None],
        dk[None],
        dv[None],
        gain.reshape(WIDTH),
        ker,
        bias.reshape(WIDTH),
    )


def solution(mesh):
    rows = P("dp", "seq", None)
    nz = mesh.shape["seq"] // (NX * NC)
    return jax.shard_map(
        functools.partial(per_device, nz, mesh.shape["dp"]),
        mesh=mesh,
        in_specs=(rows, rows, rows, P("dp", None), P(), P(), P(), rows),
        out_specs=(rows, rows, rows, rows, P(), P(), P()),
        check_vma=False,
    )
```

time: 421 us -> 75.1 us (0.18)
  blocking collectives: 113 us -> 0 us
  waiting for transfers between devices: 89.3 us -> 0 us
  other arithmetic: 70.2 us -> 1.24 us
  Pallas kernels: 0 us -> 64.3 us
  matrix products: 55.7 us -> 0 us
  local copies, waits for them, and re-layouts: 46.8 us -> 8.5 us
  starting transfers between devices: 27.8 us -> 0 us
  between operations: 15.1 us -> 0.67 us
    psum x1 -> x0, blocking collectives: 113 us -> none  [per_device(): lax.psum((gain_part, kernel_part, bias_part), ('dp', 'seq'))]
    psum x1 -> x0, waiting for transfers between devices: 83.9 us -> none  [per_device(): lax.psum((gain_part, kernel_part, bias_part), ('dp', 'seq'))]
    pallas_call x0 -> x1, Pallas kernels: none -> 64.3 us  [per_device(): pl.pallas_call(functools.partial(kernel, nz, ny), out_shape=(row, row, ro...]
    dot_general x42 -> x0, matrix products: 55.7 us -> none  [the longest x12 15.4 us: masked_logits(): jnp.einsum('qhe,khe->hqk', query_rows, key_rows, preferred_element_type=j...]
    reduce_sum x14 -> x0, other arithmetic: 51.1 us -> none  [the longest x4 29 us: per_device(): jnp.sum(jnp.where(same_taps[tap_index], conv_wide[tap_index:tap_index + f...]
    ppermute x8 -> x0, starting transfers between devices: 27.7 us -> none  [the longest x4 16 us: shifted(): return lax.ppermute(block, axis, route)]
    another operation x34 -> x0, local copies, waits for them, and re-layouts: 24.6 us -> none  [the longest x32 24.4 us: per_device(): kernel_part = jnp.stack(kernel_rows, 0)]
    slice x8 -> x0, local copies, waits for them, and re-layouts: 10.3 us -> none  [the longest x2 4.57 us: per_device(): conv_kernel[tap_index]]
  transfers between devices with their start and end apart: 9 -> 0, of which waited for: 3 -> 0; matrix products, arithmetic and copies ran while one was open for 27% -> 0% of each run, Pallas kernels for 0% -> 0%
where the time goes in v1:
time: 75.1 us; the launch traced here: 74.7 us
  Pallas kernels  64.3 us (86%)
  local copies, waits for them, and re-layouts  8.5 us (11%)
  other arithmetic  1.24 us (2%)
    pallas_call x1, Pallas kernels, per_device(): pl.pallas_call(functools.partial(kernel, nz, ny), out_shape=(row, row, ro...  64.3 us
    unnamed x19, local copies, waits for them, and re-layouts  6.6 us

profile of v1, /device:TPU:1, one launch (start us, length us, event | category | flops | bytes accessed | tf_op | source)
XLA Modules:
  0.0 74.7 jit_solution(7573641914404490557)
XLA Ops:
  0.6 0.0 copy-start.4
  0.6 1.3 %reshape.26.gain_ref = f32[1,1536]{1,0:T(1,128)} reshape(f32[1536]{0:T(1024)} %param.12) | data formatting | bytes 12288 | tf_op jit(solution)/shard_map/reshape | solution.py:654
  1.9 0.0 copy-done.4
  1.9 0.6 reshape.27.bias_ref
  2.5 64.3 %shard_map.135 = (bf16[128,1536]{1,0:T(8,128)(2,1)}, bf16[128,1536]{1,0:T(8,128)(2,1)}, bf16[128,1536]{1,0:T(8,128)(2,1)}, bf16[128,1536]{1,0:T(8,128)(2,1)}, f3...) custom-call(bf16[128,1536]{1,0:T(8,128)(2,1)} %bitcast.8, bf16[128,1536]{1,0:T(8,128)(2,1)} %bitcast.9, ...), custom_call_target="tpu_custom_call" | custom-call | tf_op jit(solution)/shard_map/pallas_call | solution.py:569
  66.9 0.0 copy-start.6
  66.9 0.7 copy-done.6
  67.6 0.0 copy-start.5
  67.6 0.6 reduce
  68.2 0.1 copy-done.5
  68.3 0.6 reduce.1
  68.9 0.0 copy-start.2
  68.9 1.8 %copy.20 = bf16[1,128,1536]{2,1,0:T(8,128)(2,1)} copy(bf16[1,128,1536]{2,1,0:T(8,128)(2,1)} %bitcast.15) | data formatting | bytes 786432
  70.7 0.0 copy-done.2
  70.7 0.0 copy-start.1
  70.7 0.7 copy.21
  71.5 0.4 copy-done.1
  71.8 0.0 copy-start
  71.8 0.7 copy.22
  72.6 0.4 copy-done
  73.0 0.0 copy-start.3
  73.0 0.7 copy.23
  73.7 0.3 copy-done.3
  74.1 0.7 copy.24
Async XLA Ops:
  0.6 1.3 %copy-start.4 = (f32[1536]{0:T(1024)S(1)}, f32[1536]{0:T(1024)}, u32[]{:S(2)}) copy-start(f32[1536]{0:T(1024)} %param.14) | copy-start | bytes 18436
  66.9 0.7 copy-start.6
  67.6 0.7 copy-start.5
  68.9 1.8 %copy-start.2 = (bf16[128,1536]{1,0:T(8,128)(2,1)S(1)}, bf16[128,1536]{1,0:T(8,128)(2,1)}, u32[]{:S(2)}) copy-start(bf16[128,1536]{1,0:T(8,128)(2,1)} %get-tuple-element.15) | copy-start | bytes 1179652
  70.7 1.1 %copy-start.1 = (bf16[128,1536]{1,0:T(8,128)(2,1)S(1)}, bf16[128,1536]{1,0:T(8,128)(2,1)}, u32[]{:S(2)}) copy-start(bf16[128,1536]{1,0:T(8,128)(2,1)} %get-tuple-element.16) | copy-start | bytes 1179652
  71.8 1.1 %copy-start = (bf16[128,1536]{1,0:T(8,128)(2,1)S(1)}, bf16[128,1536]{1,0:T(8,128)(2,1)}, u32[]{:S(2)}) copy-start(bf16[128,1536]{1,0:T(8,128)(2,1)} %get-tuple-element.17) | copy-start | bytes 1179652
  73.0 1.1 %copy-start.3 = (f32[31,1536]{1,0:T(8,128)S(1)}, f32[31,1536]{1,0:T(8,128)}, u32[]{:S(2)}) copy-start(f32[31,1536]{1,0:T(8,128)} %get-tuple-element.33) | copy-start | bytes 571396

commit v2 on v1

--- a/solution.py
+++ b/solution.py
@@ -23,9 +23,10 @@
 SCALE = HEAD_DIM ** (-0.5)
 NX = 4
 NC = 2
+GROUP = NX * NC
 TILES = PAIRS * 4
-HALF_TILES = TILES // NC
-PIECE = HALF_TILES // NX
+PIECE = TILES // GROUP
+PART = PIECE // 2
 MESH = pl.DeviceIdType.MESH
 
 
@@ -49,16 +50,17 @@
     v_hbm,
     cot_hbm,
     seg_hbm,
-    gain_ref,
-    ker_ref,
-    bias_ref,
+    gain_hbm,
+    ker_hbm,
+    bias_hbm,
     conv_hbm,
     dq_hbm,
     dk_hbm,
     dv_hbm,
-    gain_out,
-    ker_out,
-    bias_out,
+    sums_hbm,
+    gain_ref,
+    ker_ref,
+    bias_ref,
     kbuf,
     vbuf,
     qbuf,
@@ -90,14 +92,12 @@
     dq_buf,
     conv_buf,
     red,
-    core_in,
-    half,
-    xg,
-    other_in,
-    tot,
-    x_in,
-    z_in,
-    y_in,
+    r_in,
+    za_in,
+    yb_in,
+    ya_in,
+    zb_in,
+    sums,
     lsem,
     osem,
     kv_s,
@@ -108,41 +108,38 @@
     gr,
     d_s,
     d_r,
-    c_s,
-    c_r,
-    x_s,
-    x_r,
+    r_s,
+    r_r,
     z_s,
     z_r,
     y_s,
     y_r,
-    ax_s,
-    ax_r,
-    ac_s,
-    ac_r,
+    a_s,
+    a_r,
 ):
     nseq = nz * NX * NC
     me = lax.axis_index("seq")
     row = lax.axis_index("dp")
     right = lax.rem(me + 1, nseq)
     left = lax.rem(me + nseq - 1, nseq)
-    core = lax.rem(me, NC)
-    mx = lax.rem(me // NC, NX)
-    mz = me // (NC * NX)
+    mg = lax.rem(me, GROUP)
+    mz = me // GROUP
 
     def seq_dev(s):
         return (row, s)
 
-    def x_dev(k):
-        return seq_dev(mz * (NC * NX) + lax.rem(mx + k, NX) * NC + core)
+    def g_dev(k):
+        return seq_dev(mz * GROUP + lax.rem(mg + k, GROUP))
 
     def z_dev(k):
-        return seq_dev(lax.rem(mz + k, nz) * (NC * NX) + lax.rem(me, NC * NX))
+        return seq_dev(lax.rem(mz + k, nz) * GROUP + mg)
 
     def y_dev(k):
         return (lax.rem(row + k, ny), me)
 
-    core_dev = seq_dev(me + 1 - 2 * core)
+    far_g = [4, 3, 5, 2, 6, 1, 7]
+    far_z = sorted(range(1, nz), key=lambda k: -min(k, nz - k))
+    far_y = sorted(range(1, ny), key=lambda k: -min(k, ny - k))
     sides = (seq_dev(right), seq_dev(left))
 
     def remote(src, dst, s, r, dev):
@@ -165,16 +162,19 @@
                 lsem.at[4 + j],
             )
         )
+    locals_.append(pltpu.make_async_copy(gain_hbm, gain_ref, lsem.at[7]))
+    locals_.append(pltpu.make_async_copy(ker_hbm, ker_ref, lsem.at[8]))
+    locals_.append(pltpu.make_async_copy(bias_hbm, bias_ref, lsem.at[9]))
+
+    barrier = pltpu.get_barrier_semaphore()
+    partners = list(sides)
+    partners += [g_dev(k) for k in far_g]
+    partners += [z_dev(k) for k in far_z]
+    partners += [y_dev(k) for k in far_y]
+    for dev in partners:
+        pl.semaphore_signal(barrier, inc=1, device_id=dev, device_id_type=MESH)
     for copy in locals_[::-1]:
         copy.start()
-
-    barrier = pltpu.get_barrier_semaphore()
-    partners = list(sides)
-    partners += [x_dev(k) for k in range(1, NX)]
-    partners += [z_dev(k) for k in range(1, nz)]
-    partners += [y_dev(k) for k in range(1, ny)]
-    for dev in partners:
-        pl.semaphore_signal(barrier, inc=1, device_id=dev, device_id_type=MESH)
     pl.semaphore_wait(barrier, len(partners))
 
     def kv_copy(side, kv, p):
@@ -206,12 +206,15 @@
     for t in range(TAPS):
         cm[t] = jnp.where(segc[pl.ds(FR + t - 15, FR), :] == own_col, 1.0, 0.0)
 
+    for j in range(7, 10):
+        locals_[j].wait()
+
     @pl.loop(0, PAIRS)
     def _(c):
         for t in range(TAPS):
             wb[c, t] = jnp.broadcast_to(ker_ref[t : t + 1, lanes_of(c)], (8, LANES))
-        bb[c] = jnp.broadcast_to(bias_ref[:, lanes_of(c)], (8, LANES))
-        gb[c] = jnp.broadcast_to(gain_ref[:, lanes_of(c)], (8, LANES))
+        bb[c] = jnp.broadcast_to(bias_ref[lanes_of(c)].reshape(1, LANES), (8, LANES))
+        gb[c] = jnp.broadcast_to(gain_ref[lanes_of(c)].reshape(1, LANES), (8, LANES))
         kg[c] = jnp.zeros_like(kg[c])
 
     for j in range(3):
@@ -343,15 +346,34 @@
     @pl.loop(0, PAIRS)
     def _(c):
         for rg in range(4):
-            red[rg * PAIRS + c] = jnp.sum(kg[c, pl.ds(rg * 8, 8)], 1)
+            red[rg * PAIRS + c] = jnp.sum(kg[c, pl.ds(rg * 8, 8)], 1).astype(BF)
+
+    mine = pl.ds(mg * PIECE, PIECE)
+
+    def r_copy(k):
+        to = lax.rem(mg + k, GROUP)
+        return remote(
+            red.at[pl.ds(to * PIECE, PIECE)], r_in.at[mg], r_s.at[k - 1], r_r.at[k - 1], g_dev(k)
+        )
+
+    def z_copy(buf, j, k):
+        return remote(buf.at[mz], buf.at[mz], z_s.at[j, k - 1], z_r.at[j, k - 1], z_dev(k))
+
+    def y_copy(buf, j, k):
+        return remote(buf.at[row], buf.at[row], y_s.at[j, k - 1], y_r.at[j, k - 1], y_dev(k))
+
+    def a_copy(k):
+        return remote(sums.at[mine], sums.at[mine], a_s.at[k - 1], a_r.at[k - 1], g_dev(k))
+
+    def add_up(buf, count):
+        return functools.reduce(jnp.add, [buf[i].astype(F32) for i in range(count)])
+
+    for k in far_g:
+        r_copy(k).start()
+    r_in[mg] = red[mine]
 
     conv_done = pltpu.make_async_copy(conv_buf, conv_hbm, osem.at[0])
     conv_done.start()
-
-    other = (1 - core) * HALF_TILES
-    mine = core * HALF_TILES
-    core_copy = remote(red.at[pl.ds(other, HALF_TILES)], core_in, c_s, c_r, core_dev)
-    core_copy.start()
 
     def in_group(chunks, tiles):
         acc = [[None for _ in tiles] for c in chunks]
@@ -382,22 +404,6 @@
         def _(rr):
             r0 = pl.multiple_of(rr * 32 + 16, 16)
             in_group([2 * cc, 2 * cc + 1], [pl.multiple_of(r0 + 8 * i, 8) for i in range(4)])
-
-    core_copy.wait_recv()
-
-    @pl.loop(0, HALF_TILES)
-    def _(i):
-        half[i] = red[mine + i] + core_in[i]
-
-    def x_red(k):
-        to = lax.rem(mx + k, NX)
-        return remote(
-            half.at[pl.ds(to * PIECE, PIECE)], x_in.at[mx], x_s.at[k - 1], x_r.at[k - 1], x_dev(k)
-        )
-
-    for k in range(1, NX):
-        x_red(k).start()
-    x_in[mx] = half[pl.ds(mx * PIECE, PIECE)]
 
     for side in range(2):
         g_copy(side).wait_recv()
@@ -451,46 +457,42 @@
             for side in range(2):
                 d_copy(side, kv, p).start()
 
-    pl.loop(0, 3)(back)
-
-    for k in range(1, NX):
-        x_red(k).wait_recv()
-    z_in[mz] = (x_in[0] + x_in[1]) + (x_in[2] + x_in[3])
-
-    def z_copy(k):
-        return remote(z_in.at[mz], z_in.at[mz], z_s.at[k - 1], z_r.at[k - 1], z_dev(k))
-
-    def y_copy(k):
-        return remote(y_in.at[row], y_in.at[row], y_s.at[k - 1], y_r.at[k - 1], y_dev(k))
-
-    far_z = sorted(range(1, nz), key=lambda k: -min(k, nz - k))
-    far_y = sorted(range(1, ny), key=lambda k: -min(k, ny - k))
+    for k in far_g:
+        r_copy(k).wait_recv()
+    part = add_up(r_in, GROUP).astype(BF)
+    za_in[mz] = part[:PART]
+    yb_in[row] = part[PART:]
     for k in far_z:
-        z_copy(k).start()
-
-    pl.loop(3, 8)(back)
+        z_copy(za_in, 0, k).start()
+    for k in far_y:
+        y_copy(yb_in, 0, k).start()
+
+    pl.loop(0, 7)(back)
 
     for k in far_z:
-        z_copy(k).wait_recv()
-    y_in[row] = functools.reduce(jnp.add, [z_in[i] for i in range(nz)])
+        z_copy(za_in, 0, k).wait_recv()
     for k in far_y:
-        y_copy(k).start()
-
-    pl.loop(8, PAIRS)(back)
+        y_copy(yb_in, 0, k).wait_recv()
+    ya_in[row] = add_up(za_in, nz).astype(BF)
+    zb_in[mz] = add_up(yb_in, ny).astype(BF)
+    for k in far_y:
+        y_copy(ya_in, 1, k).start()
+    for k in far_z:
+        z_copy(zb_in, 1, k).start()
+
+    pl.loop(7, PAIRS)(back)
 
     dq_done = pltpu.make_async_copy(dq_buf, dq_hbm, osem.at[1])
     dq_done.start()
 
     for k in far_y:
-        y_copy(k).wait_recv()
-    xg[pl.ds(mx * PIECE, PIECE)] = functools.reduce(jnp.add, [y_in[i] for i in range(ny)])
-
-    def x_gather(k):
-        here = pl.ds(mx * PIECE, PIECE)
-        return remote(xg.at[here], xg.at[here], ax_s.at[k - 1], ax_r.at[k - 1], x_dev(k))
-
-    for k in range(1, NX):
-        x_gather(k).start()
+        y_copy(ya_in, 1, k).wait_recv()
+    for k in far_z:
+        z_copy(zb_in, 1, k).wait_recv()
+    sums[pl.ds(mg * PIECE, PART)] = add_up(ya_in, ny).astype(BF)
+    sums[pl.ds(mg * PIECE + PART, PART)] = add_up(zb_in, nz).astype(BF)
+    for k in far_g:
+        a_copy(k).start()
 
     @pl.loop(0, PAIRS)
     def _(p):
@@ -507,33 +509,10 @@
     dk_done.start()
     dv_done.start()
 
-    for k in range(1, NX):
-        x_gather(k).wait_recv()
-    gather_copy = remote(xg, other_in, ac_s, ac_r, core_dev)
-    gather_copy.start()
-    gather_copy.wait_recv()
-    factor = (ny * nseq * FR) ** (-0.5)
-
-    @pl.loop(0, HALF_TILES)
-    def _(i):
-        tot[mine + i] = xg[i]
-        tot[other + i] = other_in[i]
-
-    for c in range(PAIRS):
-        at = slice(c * LANES, (c + 1) * LANES)
-        gsum = jnp.zeros((8, LANES), F32)
-        for rg in range(4):
-            tile = tot[rg * PAIRS + c] * factor
-            if rg < 3:
-                ker_out[rg * 8 : rg * 8 + 8, at] = tile
-                gsum = gsum + tile * ker_ref[rg * 8 : rg * 8 + 8, at]
-            else:
-                ker_out[24:31, at] = tile[:7]
-                bias_out[:, at] = tile[7:]
-                gsum = gsum + jnp.concatenate(
-                    [tile[:7] * ker_ref[24:31, at], jnp.zeros((1, LANES), F32)], 0
-                )
-        gain_out[:, at] = jnp.sum(gsum, 0, keepdims=True) / gain_ref[:, at]
+    for k in far_g:
+        a_copy(k).wait_recv()
+    sums_done = pltpu.make_async_copy(sums, sums_hbm, osem.at[4])
+    sums_done.start()
 
     @pl.loop(0, PAIRS)
     def _(p):
@@ -545,19 +524,75 @@
     for side in range(2):
         x_copy(side).wait_send()
         g_copy(side).wait_send()
-    for k in range(1, NX):
-        x_red(k).wait_send()
-        x_gather(k).wait_send()
+    for k in far_g:
+        r_copy(k).wait_send()
+        a_copy(k).wait_send()
     for k in far_z:
-        z_copy(k).wait_send()
+        z_copy(za_in, 0, k).wait_send()
+        z_copy(zb_in, 1, k).wait_send()
     for k in far_y:
-        y_copy(k).wait_send()
-    core_copy.wait_send()
-    gather_copy.wait_send()
+        y_copy(yb_in, 0, k).wait_send()
+        y_copy(ya_in, 1, k).wait_send()
+    sums_done.wait()
     conv_done.wait()
     dq_done.wait()
     dk_done.wait()
     dv_done.wait()
+
+
+def finish(
+    factor,
+    conv_in,
+    dq_in,
+    dk_in,
+    dv_in,
+    sums_in,
+    gain_hbm,
+    ker_hbm,
+    conv_out,
+    dq_out,
+    dk_out,
+    dv_out,
+    gain_out,
+    ker_out,
+    bias_out,
+    gain_ref,
+    ker_ref,
+    sem,
+):
+    loads = [
+        pltpu.make_async_copy(gain_hbm, gain_ref, sem.at[4]),
+        pltpu.make_async_copy(ker_hbm, ker_ref, sem.at[5]),
+    ]
+    for copy in loads:
+        copy.start()
+    copies = [
+        pltpu.make_async_copy(a, b, sem.at[i])
+        for i, (a, b) in enumerate(
+            ((conv_in, conv_out), (dq_in, dq_out), (dk_in, dk_out), (dv_in, dv_out))
+        )
+    ]
+    for copy in copies:
+        copy.start()
+    for copy in loads:
+        copy.wait()
+    for c in range(PAIRS):
+        at = slice(c * LANES, (c + 1) * LANES)
+        gsum = jnp.zeros((8, LANES), F32)
+        for rg in range(4):
+            tile = sums_in[rg * PAIRS + c].astype(F32) * factor
+            if rg < 3:
+                ker_out[rg * 8 : rg * 8 + 8, at] = tile
+                gsum = gsum + tile * ker_ref[rg * 8 : rg * 8 + 8, at]
+            else:
+                ker_out[24:31, at] = tile[:7]
+                bias_out[at] = tile[7]
+                gsum = gsum + jnp.concatenate(
+                    [tile[:7] * ker_ref[24:31, at], jnp.zeros((1, LANES), F32)], 0
+                )
+        gain_out[at] = jnp.sum(gsum, 0) / gain_ref[at]
+    for copy in copies:
+        copy.wait()
 
 
 def per_device(nz, ny, queries, keys, values, segment_ids, norm_gain, conv_kernel, conv_bias, cot):
@@ -566,6 +601,11 @@
     any_ = pl.BlockSpec(memory_space=pl.ANY)
     whole = pl.BlockSpec(memory_space=pltpu.VMEM)
     row = jax.ShapeDtypeStruct((FR, WIDTH), BF)
+    in_hbm = functools.partial(pltpu.with_memory_space_constraint, memory_space=pltpu.HBM)
+    rows = [in_hbm(a[0]) for a in (queries, keys, values, cot)]
+    segment_ids, gain_in, ker_in, bias_in = map(
+        in_hbm, (segment_ids, norm_gain, conv_kernel, conv_bias)
+    )
     outs = pl.pallas_call(
         functools.partial(kernel, nz, ny),
         out_shape=(
@@ -573,13 +613,14 @@
             row,
             row,
             row,
-            jax.ShapeDtypeStruct((1, WIDTH), F32),
-            jax.ShapeDtypeStruct((TAPS, WIDTH), F32),
-            jax.ShapeDtypeStruct((1, WIDTH), F32),
+            jax.ShapeDtypeStruct((TILES, 8, LANES), BF),
         ),
-        in_specs=[any_] * 5 + [whole] * 3,
-        out_specs=(any_, any_, any_, any_, whole, whole, whole),
+        in_specs=[any_] * 8,
+        out_specs=(any_,) * 5,
         scratch_shapes=[
+            vmem((WIDTH,), F32),
+            vmem((TAPS, WIDTH), F32),
+            vmem((WIDTH,), F32),
             vmem((WIDE, WIDTH), BF),
             vmem((WIDE, WIDTH), BF),
             vmem((FR, WIDTH), BF),
@@ -610,17 +651,15 @@
             vmem((2, 2, FR, WIDTH), BF),
             vmem((FR, WIDTH), BF),
             vmem((FR, WIDTH), BF),
-            vmem((TILES, 8, LANES), F32),
-            vmem((HALF_TILES, 8, LANES), F32),
-            vmem((HALF_TILES, 8, LANES), F32),
-            vmem((HALF_TILES, 8, LANES), F32),
-            vmem((HALF_TILES, 8, LANES), F32),
-            vmem((TILES, 8, LANES), F32),
-            vmem((NX, PIECE, 8, LANES), F32),
-            vmem((nz, PIECE, 8, LANES), F32),
-            vmem((ny, PIECE, 8, LANES), F32),
-            dma((7,)),
-            dma((4,)),
+            vmem((TILES, 8, LANES), BF),
+            vmem((GROUP, PIECE, 8, LANES), BF),
+            vmem((nz, PART, 8, LANES), BF),
+            vmem((ny, PART, 8, LANES), BF),
+            vmem((ny, PART, 8, LANES), BF),
+            vmem((nz, PART, 8, LANES), BF),
+            vmem((TILES, 8, LANES), BF),
+            dma((10,)),
+            dma((5,)),
             dma((2, 2, PAIRS)),
             dma((2, 2, PAIRS)),
             dma((2,)),
@@ -629,42 +668,36 @@
             dma((2,)),
             dma((2, 2, PAIRS)),
             dma((2, 2, PAIRS)),
-            dma,
-            dma,
-            dma((NX - 1,)),
-            dma((NX - 1,)),
-            dma((nz - 1,)),
-            dma((nz - 1,)),
-            dma((ny - 1,)),
-            dma((ny - 1,)),
-            dma((NX - 1,)),
-            dma((NX - 1,)),
-            dma,
-            dma,
+            dma((GROUP - 1,)),
+            dma((GROUP - 1,)),
+            dma((2, nz - 1)),
+            dma((2, nz - 1)),
+            dma((2, ny - 1)),
+            dma((2, ny - 1)),
+            dma((GROUP - 1,)),
+            dma((GROUP - 1,)),
         ],
         compiler_params=pltpu.CompilerParams(
-            collective_id=0, has_side_effects=True, vmem_limit_bytes=56 * 1024 * 1024
+            collective_id=0, has_side_effects=True, vmem_limit_bytes=36 * 1024 * 1024
         ),
     )(
-        queries[0],
-        keys[0],
-        values[0],
-        cot[0],
+        *rows,
         segment_ids,
-        norm_gain.reshape(1, WIDTH),
-        conv_kernel,
-        conv_bias.reshape(1, WIDTH),
+        gain_in,
+        ker_in,
+        bias_in,
     )
-    conv_out, dq, dk, dv, gain, ker, bias = outs
-    return (
-        conv_out[None],
-        dq[None],
-        dk[None],
-        dv[None],
-        gain.reshape(WIDTH),
-        ker,
-        bias.reshape(WIDTH),
-    )
+    factor = (ny * nz * GROUP * FR) ** (-0.5)
+    vec = jax.ShapeDtypeStruct((WIDTH,), F32)
+    conv_out, dq, dk, dv, gain, ker, bias = pl.pallas_call(
+        functools.partial(finish, factor),
+        out_shape=(row, row, row, row, vec, jax.ShapeDtypeStruct((TAPS, WIDTH), F32), vec),
+        in_specs=[any_] * 4 + [whole] + [any_] * 2,
+        out_specs=(any_,) * 4 + (whole,) * 3,
+        scratch_shapes=[vmem((WIDTH,), F32), vmem((TAPS, WIDTH), F32), dma((6,))],
+        compiler_params=pltpu.CompilerParams(vmem_limit_bytes=4 * 1024 * 1024),
+    )(*outs, gain_in, ker_in)
+    return (conv_out[None], dq[None], dk[None], dv[None], gain, ker, bias)
 
 
 def solution(mesh):

time: 75.1 us -> 61.1 us (0.81)
  local copies, waits for them, and re-layouts: 8.5 us -> 0 us
  Pallas kernels: 64.3 us -> 60.3 us
  other arithmetic: 1.24 us -> 0 us
    unnamed x19 -> x0, local copies, waits for them, and re-layouts: 6.6 us -> none
    pallas_call x1, Pallas kernels: 64.3 us -> 58.3 us  [per_device(): pl.pallas_call(functools.partial(kernel, nz, ny), out_shape=(row, row, ro...]
    pallas_call x0 -> x1, Pallas kernels: none -> 1.97 us  [per_device(): pl.pallas_call(functools.partial(finish, factor), out_shape=(row, row, ro...]
    reshape x2 -> x0, local copies, waits for them, and re-layouts: 1.9 us -> none  [the longest x1 1.3 us: per_device(): norm_gain.reshape(1, WIDTH)]
    pallas_call x2 -> x0, other arithmetic: 1.24 us -> none  [per_device(): pl.pallas_call(functools.partial(kernel, nz, ny), out_shape=(row, row, ro...]
where the time goes in v2:
time: 61.1 us; the launch traced here: 60.9 us
  Pallas kernels  60.3 us (99%)
  between operations  0.64 us (1%)
    pallas_call x1, Pallas kernels, per_device(): pl.pallas_call(functools.partial(kernel, nz, ny), out_shape=(row, row, ro...  58.3 us
    pallas_call x1, Pallas kernels, per_device(): pl.pallas_call(functools.partial(finish, factor), out_shape=(row, row, ro...  1.97 us

profile of v2, /device:TPU:1, one launch (start us, length us, event | category | flops | bytes accessed | tf_op | source)
XLA Modules:
  0.0 60.9 jit_solution(6289417868921363892)
XLA Ops:
  0.6 58.3 %shard_map.135 = (bf16[128,1536]{1,0:T(8,128)(2,1)S(1)}, bf16[128,1536]{1,0:T(8,128)(2,1)S(1)}, bf16[128,1536]{1,0:T(8,128)(2,1)S(1)}, bf16[128,1536]{1,0:T(8,128)(2,1)S(1)}, bf16[48,8,128]{2,1,0:T(8,128)(2,1)S(1)}) custom-call(bf16[128,1536]{1,0:T(8,128)(2,1)} %bitcast.8, bf16[128,1536]{1,0:T(8,128)(2,1)} %bitcast.9, bf16[128,1536]{1,0:T(8,128)(2,1)} %bitcast.10, ...), custom_call_target="tpu_custom_call" | custom-call | tf_op jit(solution)/shard_map/pallas_call | solution.py:609
  58.9 2.0 %shard_map.136 = (bf16[128,1536]{1,0:T(8,128)(2,1)}, bf16[128,1536]{1,0:T(8,128)(2,1)}, bf16[128,1536]{1,0:T(8,128)(2,1)}, bf16[128,1536]{1,0:T(8,128)(2,1)}, f3...) custom-call(bf16[128,1536]{1,0:T(8,128)(2,1)S(1)} %get-tuple-element.19.conv_in, ...), custom_call_target="tpu_custom_call" | custom-call | tf_op jit(solution)/shard_map/pallas_call | solution.py:692

commit v3 on v2

--- a/solution.py
+++ b/solution.py
@@ -86,9 +86,17 @@
     gsend,
     grecv,
     kg,
+    xm,
     dkv_own,
-    dkv_send,
-    dkv_recv,
+    gnorm,
+    maskn,
+    lse,
+    lse_n,
+    delta,
+    delta_n,
+    q_n,
+    dc_buf,
+    dc_n,
     dq_buf,
     conv_buf,
     red,
@@ -106,8 +114,14 @@
     xr,
     gs,
     gr,
-    d_s,
-    d_r,
+    l_s,
+    l_r,
+    q_s,
+    q_r,
+    t_s,
+    t_r,
+    c_s,
+    c_r,
     r_s,
     r_r,
     z_s,
@@ -180,21 +194,24 @@
     def kv_copy(side, kv, p):
         src = (k_hbm, v_hbm)[kv]
         dst = (kbuf, vbuf)[kv]
-        at = 0 if side == 0 else 2 * FR
         return remote(
             src.at[:, lanes_of(p)],
-            dst.at[pl.ds(at, FR), lanes_of(p)],
-            kv_s.at[side, kv, p],
+            dst.at[pl.ds(pl.multiple_of(2 * FR * side, FR), FR), lanes_of(p)],
+            kv_s,
             kv_r.at[side, kv, p],
-            sides[side],
+            seq_dev(lax.rem(me + nseq + 1 - 2 * side, nseq)),
         )
 
-    @pl.loop(0, PAIRS)
-    def _(p):
-        for kv in range(2):
-            for side in range(2):
+    off_chip = 1 - lax.rem(me, NC)
+    for side in (off_chip, 1 - off_chip):
+
+        @pl.loop(0, PAIRS)
+        def _(p):
+            for kv in range(2):
                 kv_copy(side, kv, p).start()
 
+    zero = jnp.zeros((FR, LANES), F32)
+    acc1[...] = zero
     for j in range(3):
         locals_[4 + j].wait()
     own_row = segbuf[1]
@@ -203,6 +220,8 @@
         segc[pl.ds(j * FR, FR), :] = col
         maskb[pl.ds(j * FR, FR), :] = jnp.where(col == own_row, 0.0, NEG)
     own_col = segc[pl.ds(FR, FR), :]
+    for side in range(2):
+        maskn[side] = jnp.where(own_col == segbuf[2 * side], 0.0, NEG)
     for t in range(TAPS):
         cm[t] = jnp.where(segc[pl.ds(FR + t - 15, FR), :] == own_col, 1.0, 0.0)
 
@@ -240,16 +259,18 @@
         s = dot_nt(key, qd) * (SCALE * LOG2E) + jnp.concatenate([mask, mask], 1)
         top = jnp.max(s, 0, keepdims=True)
         e = jnp.exp2(s - top)
-        inv = 1.0 / jnp.sum(e, 0, keepdims=True)
+        total = jnp.sum(e, 0, keepdims=True)
+        inv = 1.0 / total
+        lse[p] = top + jnp.log(total) * LOG2E
         prob = (e * inv).astype(BF)
         pbuf[p] = prob
         ct = pick(dot_nn(val.T, prob)).astype(BF).astype(F32)
         ctxt[p] = ct
-        ctx[p] = ct.T
-
-    zero = jnp.zeros((FR, LANES), F32)
-    total = lax.fori_loop(0, PAIRS, lambda c, a: a + ctx[c], zero)
-    mean = jnp.broadcast_to(jnp.sum(total, 1, keepdims=True) * (1.0 / WIDTH), (FR, LANES))
+        ct = ct.T
+        ctx[p] = ct
+        acc1[...] = acc1[...] + ct
+
+    mean = jnp.broadcast_to(jnp.sum(acc1[...], 1, keepdims=True) * (1.0 / WIDTH), (FR, LANES))
     meanb[...] = mean
 
     def square(c, a):
@@ -275,18 +296,45 @@
     def g_copy(side):
         return remote(gsend.at[side], grecv.at[side], gs.at[side], gr.at[side], sides[side])
 
+    def l_copy(side):
+        return remote(lse, lse_n.at[side], l_s.at[side], l_r.at[side], sides[side])
+
+    def q_copy(side):
+        return remote(q_hbm, q_n.at[side], q_s.at[side], q_r.at[side], sides[side])
+
+    def t_copy(side):
+        return remote(delta, delta_n.at[side], t_s.at[side], t_r.at[side], sides[side])
+
+    def c_copy(side, chunk):
+        at = pl.ds(chunk * 3 * LANES, 3 * LANES)
+        return remote(
+            dc_buf.at[:, at], dc_n.at[side, :, at], c_s, c_r.at[side, chunk], sides[side]
+        )
+
     for side in range(2):
         x_copy(side).start()
+    for side in range(2):
+        l_copy(side).start()
+    for side in range(2):
+        q_copy(side).start()
     locals_[3].wait()
 
-    def conv_group(chunks, tiles):
+    def rows_of(ref, c, base, count):
+        return ref.at[c] if base is None else ref.at[c, pl.ds(base, count), :]
+
+    def conv_group(chunks, base, tiles):
+        xs_ = [rows_of(xbuf, c, base, 64) for c in chunks]
+        count = len(tiles)
         acc = [[bb[c] for _ in tiles] for c in chunks]
         for t in range(TAPS):
-            ms = [cm[t, pl.ds(r, 8), :] for r in tiles]
+            mt = rows_of(cm, t, base, 32)
+            ms = [mt[pl.ds(r, 8), :] for r in tiles]
             for j, c in enumerate(chunks):
                 w = wb[c, t]
                 for i, r in enumerate(tiles):
-                    acc[j][i] = acc[j][i] + w * (ms[i] * xbuf[c, pl.ds(r + t + 1, 8), :])
+                    x = ms[i] * xs_[j][pl.ds(r + t + 1, 8), :]
+                    xm[t, j * count + i] = x
+                    acc[j][i] = acc[j][i] + w * x
         gr_ = []
         for j, c in enumerate(chunks):
             gr_.append([])
@@ -295,40 +343,37 @@
                 sig = 1.0 / (1.0 + jnp.exp(-a))
                 acc[j][i] = a * sig
                 gr_[j].append(sig * (1.0 + a * (1.0 - sig)))
-        bias_sum = []
         for j, c in enumerate(chunks):
             for h in range(0, len(tiles), 2):
-                r = tiles[h]
+                at = tiles[h] if base is None else base + tiles[h]
                 out = jnp.concatenate(acc[j][h : h + 2], 0).astype(BF)
-                conv_buf[pl.ds(r, 16), lanes_of(c)] = out
+                conv_buf[pl.ds(at, 16), lanes_of(c)] = out
                 g = jnp.concatenate(gr_[j][h : h + 2], 0)
-                g = (g * cotbuf[pl.ds(r, 16), lanes_of(c)].astype(F32)).astype(BF)
-                if isinstance(r, int) and r == 0:
+                g = (g * cotbuf[pl.ds(at, 16), lanes_of(c)].astype(F32)).astype(BF)
+                if base is None and h == 0:
                     gsend[1, c] = g
-                elif isinstance(r, int) and r == FR - 16:
+                elif base is None:
                     gsend[0, c] = g
                 g = g.astype(F32)
-                gbuf[c, pl.ds(r + 16, 16), :] = g
+                gbuf[c, pl.ds(at + 16, 16), :] = g
                 gr_[j][h] = g[:8]
                 gr_[j][h + 1] = g[8:]
             kg[c, TAPS] = kg[c, TAPS] + functools.reduce(jnp.add, gr_[j])
         for t in range(TAPS):
-            ms = [cm[t, pl.ds(r, 8), :] for r in tiles]
             for j, c in enumerate(chunks):
-                terms = [
-                    gr_[j][i] * (ms[i] * xbuf[c, pl.ds(r + t + 1, 8), :])
-                    for i, r in enumerate(tiles)
-                ]
+                terms = [gr_[j][i] * xm[t, j * count + i] for i in range(count)]
                 kg[c, t] = kg[c, t] + functools.reduce(jnp.add, terms)
 
     edges = [0, 8, FR - 16, FR - 8]
+    tap_row = lax.broadcasted_iota(jnp.int32, (TAPS + 1, TAPS * 8 + 8), 0)
+    sub_row = lax.broadcasted_iota(jnp.int32, (TAPS + 1, TAPS * 8 + 8), 1) // 8
+    rows8 = jnp.where(tap_row == sub_row, 1.0, 0.0).astype(BF)
 
     @pl.loop(0, PAIRS // 2)
     def _(cc):
         @pl.loop(0, 3)
         def _(rr):
-            r0 = pl.multiple_of(rr * 32 + 16, 16)
-            conv_group([2 * cc, 2 * cc + 1], [pl.multiple_of(r0 + 8 * i, 8) for i in range(4)])
+            conv_group([2 * cc, 2 * cc + 1], pl.multiple_of(rr * 32 + 16, 16), [0, 8, 16, 24])
 
     for side in range(2):
         x_copy(side).wait_recv()
@@ -338,32 +383,34 @@
         for c in (2 * cc, 2 * cc + 1):
             xbuf[c, pl.ds(0, 16), :] = xrecv[0, c].astype(F32)
             xbuf[c, pl.ds(FR + 16, 16), :] = xrecv[1, c].astype(F32)
-        conv_group([2 * cc, 2 * cc + 1], edges)
+        conv_group([2 * cc, 2 * cc + 1], None, edges)
+        for c in (2 * cc, 2 * cc + 1):
+            whole = kg[c].reshape(TAPS * 8 + 8, LANES)
+            high = whole.astype(BF)
+            low_part = (whole - high.astype(F32)).astype(BF)
+            total = dot_nn(rows8, high) + dot_nn(rows8, low_part)
+            for rg in range(4):
+                red[rg * PAIRS + c] = total[rg * 8 : rg * 8 + 8].astype(BF)
 
     for side in range(2):
         g_copy(side).start()
-
-    @pl.loop(0, PAIRS)
-    def _(c):
-        for rg in range(4):
-            red[rg * PAIRS + c] = jnp.sum(kg[c, pl.ds(rg * 8, 8)], 1).astype(BF)
 
     mine = pl.ds(mg * PIECE, PIECE)
 
     def r_copy(k):
         to = lax.rem(mg + k, GROUP)
         return remote(
-            red.at[pl.ds(to * PIECE, PIECE)], r_in.at[mg], r_s.at[k - 1], r_r.at[k - 1], g_dev(k)
+            red.at[pl.ds(to * PIECE, PIECE)], r_in.at[mg], r_s, r_r.at[k - 1], g_dev(k)
         )
 
     def z_copy(buf, j, k):
-        return remote(buf.at[mz], buf.at[mz], z_s.at[j, k - 1], z_r.at[j, k - 1], z_dev(k))
+        return remote(buf.at[mz], buf.at[mz], z_s.at[j], z_r.at[j, k - 1], z_dev(k))
 
     def y_copy(buf, j, k):
-        return remote(buf.at[row], buf.at[row], y_s.at[j, k - 1], y_r.at[j, k - 1], y_dev(k))
+        return remote(buf.at[row], buf.at[row], y_s.at[j], y_r.at[j, k - 1], y_dev(k))
 
     def a_copy(k):
-        return remote(sums.at[mine], sums.at[mine], a_s.at[k - 1], a_r.at[k - 1], g_dev(k))
+        return remote(sums.at[mine], sums.at[mine], a_s, a_r.at[k - 1], g_dev(k))
 
     def add_up(buf, count):
         return functools.reduce(jnp.add, [buf[i].astype(F32) for i in range(count)])
@@ -375,25 +422,28 @@
     conv_done = pltpu.make_async_copy(conv_buf, conv_hbm, osem.at[0])
     conv_done.start()
 
-    def in_group(chunks, tiles):
+    def in_group(chunks, base, tiles):
+        gs_ = [rows_of(gbuf, c, base, 64) for c in chunks]
         acc = [[None for _ in tiles] for c in chunks]
         for u in range(TAPS):
-            ms = [cm[u, pl.ds(r, 8), :] for r in tiles]
+            mt = rows_of(cm, u, base, 32)
+            ms = [mt[pl.ds(r, 8), :] for r in tiles]
             for j, c in enumerate(chunks):
                 w = wb[c, TAPS - 1 - u]
                 for i, r in enumerate(tiles):
-                    term = w * (ms[i] * gbuf[c, pl.ds(r + u + 1, 8), :])
+                    term = w * (ms[i] * gs_[j][pl.ds(r + u + 1, 8), :])
                     acc[j][i] = term if u == 0 else acc[j][i] + term
         for i, r in enumerate(tiles):
-            s1 = acc1[pl.ds(r, 8), :]
-            s2 = acc2[pl.ds(r, 8), :]
+            at = pl.ds(r if base is None else base + r, 8)
+            s1 = acc1[at, :]
+            s2 = acc2[at, :]
             for j, c in enumerate(chunks):
                 g = acc[j][i] * gb[c]
-                dkv_own[0, c, pl.ds(r, 8), :] = g
+                gnorm[c, at, :] = g
                 s1 = s1 + g
-                s2 = s2 + g * ctx[c, pl.ds(r, 8), :]
-            acc1[pl.ds(r, 8), :] = s1
-            acc2[pl.ds(r, 8), :] = s2
+                s2 = s2 + g * ctx[c, at, :]
+            acc1[at, :] = s1
+            acc2[at, :] = s2
 
     acc1[...] = zero
     acc2[...] = zero
@@ -402,8 +452,7 @@
     def _(cc):
         @pl.loop(0, 3)
         def _(rr):
-            r0 = pl.multiple_of(rr * 32 + 16, 16)
-            in_group([2 * cc, 2 * cc + 1], [pl.multiple_of(r0 + 8 * i, 8) for i in range(4)])
+            in_group([2 * cc, 2 * cc + 1], pl.multiple_of(rr * 32 + 16, 16), [0, 8, 16, 24])
 
     for side in range(2):
         g_copy(side).wait_recv()
@@ -413,49 +462,7 @@
         for c in (2 * cc, 2 * cc + 1):
             gbuf[c, pl.ds(0, 16), :] = grecv[0, c].astype(F32)
             gbuf[c, pl.ds(FR + 16, 16), :] = grecv[1, c].astype(F32)
-        in_group([2 * cc, 2 * cc + 1], edges)
-
-    acc1[...] = jnp.broadcast_to(jnp.sum(acc1[...], 1, keepdims=True) * (1.0 / WIDTH), (FR, LANES))
-    acc2[...] = jnp.broadcast_to(jnp.sum(acc2[...], 1, keepdims=True) * (1.0 / WIDTH), (FR, LANES))
-
-    def d_copy(side, kv, p):
-        return remote(
-            dkv_send.at[side, kv, :, lanes_of(p)],
-            dkv_recv.at[side, kv, :, lanes_of(p)],
-            d_s.at[side, kv, p],
-            d_r.at[side, kv, p],
-            sides[side],
-        )
-
-    def back(p):
-        dc = (dkv_own[0, p] - acc1[...] - ctx[p] * acc2[...]) * invb[...]
-        dc = dc.astype(BF)
-        prod = dc.astype(F32).T * ctxt[p]
-        delta = jnp.concatenate(
-            [
-                jnp.sum(prod[:HEAD_DIM], 0, keepdims=True),
-                jnp.sum(prod[HEAD_DIM:], 0, keepdims=True),
-            ],
-            1,
-        )
-        key = kbuf[:, lanes_of(p)]
-        val = vbuf[:, lanes_of(p)]
-        dcd = diag(dc)
-        qd = diag(qbuf[:, lanes_of(p)])
-        prob = pbuf[p]
-        dp = dot_nt(val, dcd)
-        ds = (prob.astype(F32) * ((dp - delta) * SCALE)).astype(BF)
-        dv = dot_nn(prob, dcd)
-        dk = dot_nn(ds, qd)
-        dq = pick(dot_nn(key.T, ds)).T
-        dq_buf[:, lanes_of(p)] = dq.astype(BF)
-        for kv, d in enumerate((dk, dv)):
-            dkv_send[1, kv, :, lanes_of(p)] = d[:FR].astype(BF)
-            dkv_own[kv, p] = d[FR : 2 * FR]
-            dkv_send[0, kv, :, lanes_of(p)] = d[2 * FR :].astype(BF)
-        for kv in range(2):
-            for side in range(2):
-                d_copy(side, kv, p).start()
+        in_group([2 * cc, 2 * cc + 1], None, edges)
 
     for k in far_g:
         r_copy(k).wait_recv()
@@ -466,6 +473,56 @@
         z_copy(za_in, 0, k).start()
     for k in far_y:
         y_copy(yb_in, 0, k).start()
+
+    acc1[...] = jnp.broadcast_to(jnp.sum(acc1[...], 1, keepdims=True) * (1.0 / WIDTH), (FR, LANES))
+    acc2[...] = jnp.broadcast_to(jnp.sum(acc2[...], 1, keepdims=True) * (1.0 / WIDTH), (FR, LANES))
+
+    @pl.loop(0, PAIRS)
+    def _(p):
+        dc = (gnorm[p] - acc1[...] - ctx[p] * acc2[...]) * invb[...]
+        dc = dc.astype(BF)
+        dc_buf[:, lanes_of(p)] = dc
+        prod = dc.astype(F32).T * ctxt[p]
+        delta[p] = jnp.concatenate(
+            [
+                jnp.sum(prod[:HEAD_DIM], 0, keepdims=True),
+                jnp.sum(prod[HEAD_DIM:], 0, keepdims=True),
+            ],
+            1,
+        )
+
+    for side in range(2):
+        t_copy(side).start()
+    for chunk in range(4):
+        for side in range(2):
+            c_copy(side, chunk).start()
+
+    def back(p):
+        key = kbuf[:, lanes_of(p)]
+        val = vbuf[:, lanes_of(p)]
+        dcd = diag(dc_buf[:, lanes_of(p)])
+        qd = diag(qbuf[:, lanes_of(p)])
+        prob = pbuf[p]
+        dp = dot_nt(val, dcd)
+        ds = (prob.astype(F32) * ((dp - delta[p]) * SCALE)).astype(BF)
+        dkv_own[0, p] = dot_nn(ds[FR : 2 * FR], qd)
+        dkv_own[1, p] = dot_nn(prob[FR : 2 * FR], dcd)
+        dq_buf[:, lanes_of(p)] = pick(dot_nn(key.T, ds)).T.astype(BF)
+
+    def back_near(p):
+        key = kbuf[pl.ds(FR, FR), lanes_of(p)]
+        val = vbuf[pl.ds(FR, FR), lanes_of(p)]
+        qd = jnp.concatenate([diag(q_n[side, :, lanes_of(p)]) for side in range(2)], 0)
+        dcd = jnp.concatenate([diag(dc_n[side, :, lanes_of(p)]) for side in range(2)], 0)
+        shift = jnp.concatenate([lse_n[side, p] for side in range(2)], 1)
+        dlt = jnp.concatenate([delta_n[side, p] for side in range(2)], 1)
+        mask = jnp.concatenate([maskn[0], maskn[0], maskn[1], maskn[1]], 1)
+        prob = jnp.exp2(dot_nt(key, qd) * (SCALE * LOG2E) + (mask - shift))
+        ds = (prob * ((dot_nt(val, dcd) - dlt) * SCALE)).astype(BF)
+        dk = dkv_own[0, p] + dot_nn(ds, qd)
+        dv = dkv_own[1, p] + dot_nn(prob.astype(BF), dcd)
+        kbuf[pl.ds(FR, FR), lanes_of(p)] = dk.astype(BF)
+        vbuf[pl.ds(FR, FR), lanes_of(p)] = dv.astype(BF)
 
     pl.loop(0, 7)(back)
 
@@ -485,6 +542,15 @@
     dq_done = pltpu.make_async_copy(dq_buf, dq_hbm, osem.at[1])
     dq_done.start()
 
+    for side in range(2):
+        l_copy(side).wait_recv()
+        q_copy(side).wait_recv()
+        t_copy(side).wait_recv()
+    for chunk in range(2):
+        for side in range(2):
+            c_copy(side, chunk).wait_recv()
+    pl.loop(0, 5)(back_near)
+
     for k in far_y:
         y_copy(ya_in, 1, k).wait_recv()
     for k in far_z:
@@ -494,15 +560,10 @@
     for k in far_g:
         a_copy(k).start()
 
-    @pl.loop(0, PAIRS)
-    def _(p):
-        for kv in range(2):
-            for side in range(2):
-                d_copy(side, kv, p).wait_recv()
-            d = dkv_own[kv, p]
-            d = d + dkv_recv[0, kv, :, lanes_of(p)].astype(F32)
-            d = d + dkv_recv[1, kv, :, lanes_of(p)].astype(F32)
-            (kbuf, vbuf)[kv][pl.ds(FR, FR), lanes_of(p)] = d.astype(BF)
+    for chunk in range(2, 4):
+        for side in range(2):
+            c_copy(side, chunk).wait_recv()
+    pl.loop(5, PAIRS)(back_near)
 
     dk_done = pltpu.make_async_copy(kbuf.at[own, :], dk_hbm, osem.at[2])
     dv_done = pltpu.make_async_copy(vbuf.at[own, :], dv_hbm, osem.at[3])
@@ -514,25 +575,23 @@
     sums_done = pltpu.make_async_copy(sums, sums_hbm, osem.at[4])
     sums_done.start()
 
-    @pl.loop(0, PAIRS)
-    def _(p):
-        for kv in range(2):
-            for side in range(2):
-                kv_copy(side, kv, p).wait_send()
-                d_copy(side, kv, p).wait_send()
-
+    def sent(buf, sem):
+        remote(buf, buf, sem, sem, sides[0]).wait_send()
+
+    sent(pbuf.at[pl.ds(0, 8)], kv_s)
+    sent(pbuf.at[pl.ds(0, 4)], c_s)
     for side in range(2):
         x_copy(side).wait_send()
         g_copy(side).wait_send()
-    for k in far_g:
-        r_copy(k).wait_send()
-        a_copy(k).wait_send()
-    for k in far_z:
-        z_copy(za_in, 0, k).wait_send()
-        z_copy(zb_in, 1, k).wait_send()
-    for k in far_y:
-        y_copy(yb_in, 0, k).wait_send()
-        y_copy(ya_in, 1, k).wait_send()
+        l_copy(side).wait_send()
+        q_copy(side).wait_send()
+        t_copy(side).wait_send()
+    others = pl.ds(0, GROUP - 1)
+    sent(r_in.at[others], r_s)
+    sent(r_in.at[others], a_s)
+    for j in range(2):
+        sent(za_in.at[pl.ds(0, nz - 1)], z_s.at[j])
+        sent(yb_in.at[pl.ds(0, ny - 1)], y_s.at[j])
     sums_done.wait()
     conv_done.wait()
     dq_done.wait()
@@ -646,9 +705,17 @@
             vmem((2, PAIRS, 16, LANES), BF),
             vmem((2, PAIRS, 16, LANES), BF),
             vmem((PAIRS, 32, 8, LANES), F32),
+            vmem((TAPS, 8, 8, LANES), F32),
             vmem((2, PAIRS, FR, LANES), F32),
-            vmem((2, 2, FR, WIDTH), BF),
-            vmem((2, 2, FR, WIDTH), BF),
+            vmem((PAIRS, FR, LANES), F32),
+            vmem((2, FR, LANES), F32),
+            vmem((PAIRS, 1, 2 * LANES), F32),
+            vmem((2, PAIRS, 1, 2 * LANES), F32),
+            vmem((PAIRS, 1, 2 * LANES), F32),
+            vmem((2, PAIRS, 1, 2 * LANES), F32),
+            vmem((2, FR, WIDTH), BF),
+            vmem((FR, WIDTH), BF),
+            vmem((2, FR, WIDTH), BF),
             vmem((FR, WIDTH), BF),
             vmem((FR, WIDTH), BF),
             vmem((TILES, 8, LANES), BF),
@@ -660,21 +727,27 @@
             vmem((TILES, 8, LANES), BF),
             dma((10,)),
             dma((5,)),
+            dma,
             dma((2, 2, PAIRS)),
-            dma((2, 2, PAIRS)),
-            dma((2,)),
-            dma((2,)),
-            dma((2,)),
-            dma((2,)),
-            dma((2, 2, PAIRS)),
-            dma((2, 2, PAIRS)),
+            dma((2,)),
+            dma((2,)),
+            dma((2,)),
+            dma((2,)),
+            dma((2,)),
+            dma((2,)),
+            dma((2,)),
+            dma((2,)),
+            dma((2,)),
+            dma((2,)),
+            dma,
+            dma((2, 4)),
+            dma,
             dma((GROUP - 1,)),
-            dma((GROUP - 1,)),
+            dma((2,)),
             dma((2, nz - 1)),
-            dma((2, nz - 1)),
+            dma((2,)),
             dma((2, ny - 1)),
-            dma((2, ny - 1)),
-            dma((GROUP - 1,)),
+            dma,
             dma((GROUP - 1,)),
         ],
         compiler_params=pltpu.CompilerParams(

time: 61.1 us -> 57 us (0.933)
  Pallas kernels: 60.3 us -> 56.2 us
    pallas_call x1, Pallas kernels: 58.3 us -> 54.2 us  [per_device(): pl.pallas_call(functools.partial(kernel, nz, ny), out_shape=(row, row, ro...]
where the time goes in v3:
time: 57 us; the launch traced here: 56.8 us
  Pallas kernels  56.2 us (99%)
  between operations  0.64 us (1%)
    pallas_call x1, Pallas kernels, per_device(): pl.pallas_call(functools.partial(kernel, nz, ny), out_shape=(row, row, ro...  54.2 us
    pallas_call x1, Pallas kernels, per_device(): pl.pallas_call(functools.partial(finish, factor), out_shape=(row, row, ro...  1.97 us

profile of v3, /device:TPU:1, one launch (start us, length us, event | category | flops | bytes accessed | tf_op | source)
XLA Modules:
  0.0 56.8 jit_solution(4996582499417365744)
XLA Ops:
  0.6 54.2 %shard_map.135 = (bf16[128,1536]{1,0:T(8,128)(2,1)S(1)}, bf16[128,1536]{1,0:T(8,128)(2,1)S(1)}, bf16[128,1536]{1,0:T(8,128)(2,1)S(1)}, bf16[128,1536]{1,0:T(8,128)(2,1)S(1)}, bf16[48,8,128]{2,1,0:T(8,128)(2,1)S(1)}) custom-call(bf16[128,1536]{1,0:T(8,128)(2,1)} %bitcast.8, bf16[128,1536]{1,0:T(8,128)(2,1)} %bitcast.9, bf16[128,1536]{1,0:T(8,128)(2,1)} %bitcast.10, ...), custom_call_target="tpu_custom_call" | custom-call | tf_op jit(solution)/shard_map/pallas_call | solution.py:668
  54.9 2.0 %shard_map.136 = (bf16[128,1536]{1,0:T(8,128)(2,1)}, bf16[128,1536]{1,0:T(8,128)(2,1)}, bf16[128,1536]{1,0:T(8,128)(2,1)}, bf16[128,1536]{1,0:T(8,128)(2,1)}, f3...) custom-call(bf16[128,1536]{1,0:T(8,128)(2,1)S(1)} %get-tuple-element.19.conv_in, ...), custom_call_target="tpu_custom_call" | custom-call | tf_op jit(solution)/shard_map/pallas_call | solution.py:765

commit v4 on v3

--- a/solution.py
+++ b/solution.py
@@ -155,6 +155,10 @@
     far_z = sorted(range(1, nz), key=lambda k: -min(k, nz - k))
     far_y = sorted(range(1, ny), key=lambda k: -min(k, ny - k))
     sides = (seq_dev(right), seq_dev(left))
+    has_right = me < nseq - 1
+    has_left = me > 0
+    sends = (has_right, has_left)
+    takes = (has_left, has_right)
 
     def remote(src, dst, s, r, dev):
         return pltpu.make_async_remote_copy(
@@ -196,19 +200,32 @@
         dst = (kbuf, vbuf)[kv]
         return remote(
             src.at[:, lanes_of(p)],
-            dst.at[pl.ds(pl.multiple_of(2 * FR * side, FR), FR), lanes_of(p)],
-            kv_s,
+            dst.at[pl.ds(2 * FR * side, FR), lanes_of(p)],
+            kv_s.at[side],
             kv_r.at[side, kv, p],
-            seq_dev(lax.rem(me + nseq + 1 - 2 * side, nseq)),
+            sides[side],
         )
 
-    off_chip = 1 - lax.rem(me, NC)
-    for side in (off_chip, 1 - off_chip):
-
-        @pl.loop(0, PAIRS)
-        def _(p):
-            for kv in range(2):
-                kv_copy(side, kv, p).start()
+    for side in range(2):
+
+        @pl.when(sends[side])
+        def _(side=side):
+            @pl.loop(0, PAIRS)
+            def _(p):
+                for kv in range(2):
+                    kv_copy(side, kv, p).start()
+
+        @pl.when(jnp.logical_not(takes[side]))
+        def _(side=side):
+            rows = pl.ds(2 * FR * side, FR)
+            kbuf[rows, :] = jnp.zeros((FR, WIDTH), BF)
+            vbuf[rows, :] = jnp.zeros((FR, WIDTH), BF)
+            q_n[side] = jnp.zeros((FR, WIDTH), BF)
+            dc_n[side] = jnp.zeros((FR, WIDTH), BF)
+            lse_n[side] = jnp.zeros((PAIRS, 1, 2 * LANES), F32)
+            delta_n[side] = jnp.zeros((PAIRS, 1, 2 * LANES), F32)
+            xrecv[side] = jnp.zeros((PAIRS, 16, LANES), BF)
+            grecv[side] = jnp.zeros((PAIRS, 16, LANES), BF)
 
     zero = jnp.zeros((FR, LANES), F32)
     acc1[...] = zero
@@ -249,9 +266,13 @@
 
     @pl.loop(0, PAIRS)
     def _(p):
-        for kv in range(2):
-            for side in range(2):
-                kv_copy(side, kv, p).wait_recv()
+        for side in range(2):
+
+            @pl.when(takes[side])
+            def _(side=side):
+                for kv in range(2):
+                    kv_copy(side, kv, p).wait_recv()
+
         key = kbuf[:, lanes_of(p)]
         val = vbuf[:, lanes_of(p)]
         qd = diag(qbuf[:, lanes_of(p)])
@@ -308,15 +329,23 @@
     def c_copy(side, chunk):
         at = pl.ds(chunk * 3 * LANES, 3 * LANES)
         return remote(
-            dc_buf.at[:, at], dc_n.at[side, :, at], c_s, c_r.at[side, chunk], sides[side]
+            dc_buf.at[:, at], dc_n.at[side, :, at], c_s.at[side], c_r.at[side, chunk], sides[side]
         )
 
-    for side in range(2):
-        x_copy(side).start()
-    for side in range(2):
-        l_copy(side).start()
-    for side in range(2):
-        q_copy(side).start()
+    def each(when, *what):
+        for side in range(2):
+
+            @pl.when(when[side])
+            def _(side=side):
+                for act in what:
+                    act(side)
+
+    each(
+        sends,
+        lambda side: x_copy(side).start(),
+        lambda side: l_copy(side).start(),
+        lambda side: q_copy(side).start(),
+    )
     locals_[3].wait()
 
     def rows_of(ref, c, base, count):
@@ -375,8 +404,7 @@
         def _(rr):
             conv_group([2 * cc, 2 * cc + 1], pl.multiple_of(rr * 32 + 16, 16), [0, 8, 16, 24])
 
-    for side in range(2):
-        x_copy(side).wait_recv()
+    each(takes, lambda side: x_copy(side).wait_recv())
 
     @pl.loop(0, PAIRS // 2)
     def _(cc):
@@ -392,8 +420,7 @@
             for rg in range(4):
                 red[rg * PAIRS + c] = total[rg * 8 : rg * 8 + 8].astype(BF)
 
-    for side in range(2):
-        g_copy(side).start()
+    each(sends, lambda side: g_copy(side).start())
 
     mine = pl.ds(mg * PIECE, PIECE)
 
@@ -454,8 +481,7 @@
         def _(rr):
             in_group([2 * cc, 2 * cc + 1], pl.multiple_of(rr * 32 + 16, 16), [0, 8, 16, 24])
 
-    for side in range(2):
-        g_copy(side).wait_recv()
+    each(takes, lambda side: g_copy(side).wait_recv())
 
     @pl.loop(0, PAIRS // 2)
     def _(cc):
@@ -491,11 +517,11 @@
             1,
         )
 
-    for side in range(2):
-        t_copy(side).start()
-    for chunk in range(4):
-        for side in range(2):
-            c_copy(side, chunk).start()
+    each(
+        sends,
+        lambda side: t_copy(side).start(),
+        *[lambda side, chunk=chunk: c_copy(side, chunk).start() for chunk in range(4)],
+    )
 
     def back(p):
         key = kbuf[:, lanes_of(p)]
@@ -542,13 +568,14 @@
     dq_done = pltpu.make_async_copy(dq_buf, dq_hbm, osem.at[1])
     dq_done.start()
 
-    for side in range(2):
-        l_copy(side).wait_recv()
-        q_copy(side).wait_recv()
-        t_copy(side).wait_recv()
-    for chunk in range(2):
-        for side in range(2):
-            c_copy(side, chunk).wait_recv()
+    each(
+        takes,
+        lambda side: l_copy(side).wait_recv(),
+        lambda side: q_copy(side).wait_recv(),
+        lambda side: t_copy(side).wait_recv(),
+        lambda side: c_copy(side, 0).wait_recv(),
+        lambda side: c_copy(side, 1).wait_recv(),
+    )
     pl.loop(0, 5)(back_near)
 
     for k in far_y:
@@ -560,9 +587,11 @@
     for k in far_g:
         a_copy(k).start()
 
-    for chunk in range(2, 4):
-        for side in range(2):
-            c_copy(side, chunk).wait_recv()
+    each(
+        takes,
+        lambda side: c_copy(side, 2).wait_recv(),
+        lambda side: c_copy(side, 3).wait_recv(),
+    )
     pl.loop(5, PAIRS)(back_near)
 
     dk_done = pltpu.make_async_copy(kbuf.at[own, :], dk_hbm, osem.at[2])
@@ -578,14 +607,16 @@
     def sent(buf, sem):
         remote(buf, buf, sem, sem, sides[0]).wait_send()
 
-    sent(pbuf.at[pl.ds(0, 8)], kv_s)
-    sent(pbuf.at[pl.ds(0, 4)], c_s)
-    for side in range(2):
-        x_copy(side).wait_send()
-        g_copy(side).wait_send()
-        l_copy(side).wait_send()
-        q_copy(side).wait_send()
-        t_copy(side).wait_send()
+    each(
+        sends,
+        lambda side: sent(pbuf.at[pl.ds(0, 4)], kv_s.at[side]),
+        lambda side: sent(dc_buf, c_s.at[side]),
+        lambda side: x_copy(side).wait_send(),
+        lambda side: g_copy(side).wait_send(),
+        lambda side: l_copy(side).wait_send(),
+        lambda side: q_copy(side).wait_send(),
+        lambda side: t_copy(side).wait_send(),
+    )
     others = pl.ds(0, GROUP - 1)
     sent(r_in.at[others], r_s)
     sent(r_in.at[others], a_s)
@@ -727,7 +758,7 @@
             vmem((TILES, 8, LANES), BF),
             dma((10,)),
             dma((5,)),
-            dma,
+            dma((2,)),
             dma((2, 2, PAIRS)),
             dma((2,)),
             dma((2,)),
@@ -739,7 +770,7 @@
             dma((2,)),
             dma((2,)),
             dma((2,)),
-            dma,
+            dma((2,)),
             dma((2, 4)),
             dma,
             dma((GROUP - 1,)),

time: 57 us -> 56.2 us (0.986)
  Pallas kernels: 56.2 us -> 55.4 us
    pallas_call x1, Pallas kernels: 54.2 us -> 53.4 us  [per_device(): pl.pallas_call(functools.partial(kernel, nz, ny), out_shape=(row, row, ro...]
where the time goes in v4:
time: 56.2 us; the launch traced here: 56 us
  Pallas kernels  55.4 us (99%)
  between operations  0.64 us (1%)
    pallas_call x1, Pallas kernels, per_device(): pl.pallas_call(functools.partial(kernel, nz, ny), out_shape=(row, row, ro...  53.4 us
    pallas_call x1, Pallas kernels, per_device(): pl.pallas_call(functools.partial(finish, factor), out_shape=(row, row, ro...  1.97 us

profile of v4, /device:TPU:1, one launch (start us, length us, event | category | flops | bytes accessed | tf_op | source)
XLA Modules:
  0.0 56.0 jit_solution(4305608088383791436)
XLA Ops:
  0.6 53.4 %shard_map.135 = (bf16[128,1536]{1,0:T(8,128)(2,1)S(1)}, bf16[128,1536]{1,0:T(8,128)(2,1)S(1)}, bf16[128,1536]{1,0:T(8,128)(2,1)S(1)}, bf16[128,1536]{1,0:T(8,128)(2,1)S(1)}, bf16[48,8,128]{2,1,0:T(8,128)(2,1)S(1)}) custom-call(bf16[128,1536]{1,0:T(8,128)(2,1)} %bitcast.8, bf16[128,1536]{1,0:T(8,128)(2,1)} %bitcast.9, bf16[128,1536]{1,0:T(8,128)(2,1)} %bitcast.10, ...), custom_call_target="tpu_custom_call" | custom-call | tf_op jit(solution)/shard_map/pallas_call | solution.py:699
  54.0 2.0 %shard_map.136 = (bf16[128,1536]{1,0:T(8,128)(2,1)}, bf16[128,1536]{1,0:T(8,128)(2,1)}, bf16[128,1536]{1,0:T(8,128)(2,1)}, bf16[128,1536]{1,0:T(8,128)(2,1)}, f3...) custom-call(bf16[128,1536]{1,0:T(8,128)(2,1)S(1)} %get-tuple-element.19.conv_in, ...), custom_call_target="tpu_custom_call" | custom-call | tf_op jit(solution)/shard_map/pallas_call | solution.py:796
